TPU v7x, 256 devices: a whole 4x4x8 slice. The times are simulated.
256 devices in a mesh: row: 8 (over x, core), col: 32 (over y, z).
Axes of the slice: x: 4, y: 4, z: 8, core: 2. Of those that a mesh axis runs over, the one named last changes fastest.
Arguments:
- src_coords: int32 [3, 131072], P(None, 'row'), may hold values from 0 to 51
- tgt_coords: int32 [3, 262144], P(None, 'col'), may hold values from 0 to 51
- src_mass: int32 [131072], P('row'), may hold values from 1 to 298
- tgt_mass: int32 [262144], P('col'), may hold values from 1 to 298
- tgt_start: float32 [262144], P('col'), may hold values from -10 to 170
- kept_src: int32 [8, 32, 64], P('row', 'col'), may hold values from 0 to 127, as said below
- kept_tgt: int32 [8, 32, 64], P('row', 'col'), may hold values from 0 to 63, as said below
- kept_count: int32 [8, 32], P('row', 'col'), may hold values from 1 to 64, as said below
Outputs:
- src_potential: float32 [131072], P('row')
- tgt_potential: float32 [262144], P('col')
Inputs may be any that keep to these rules, and one draw needn't show every extreme that they name: `kept_src`: every source tile lies in a live pair of some device of its row block. Slots at or past a device's count hold pairs that are not live. `kept_tgt`: every target tile lies in a live pair of some device of its column block. `kept_count`: some device has exactly 64 live slots in every draw.
All inputs are finite; a program needn't handle non-finite values.
Results may differ from a plain program's by a relative error of at most 0.0001.
Values sent between devices are 32-bit elements; how exact they have to be, the bound alone decides.
No kernel may reach another device: no remote copies, remote signals or barrier semaphores. Data moves between devices by JAX's collectives and lax.ppermute only.
A program may use at most 64 MiB of HBM per device.

v0:
```python
import functools

import jax
import jax.numpy as jnp
from jax import lax
from jax.experimental import pallas as pl
from jax.experimental.pallas import tpu as pltpu
from jax.sharding import PartitionSpec as P

ITERS = 3
NONE = -1.0e30
LOG2E = 1.4426950408889634
LN2 = 0.6931471805599453
COST = 0.05 * LOG2E
SLOTS = 64
GROUP = 16
F32 = jnp.float32


def lse(parts):
    top = functools.reduce(jnp.maximum, parts)
    terms = [jnp.exp(p - top) for p in parts]
    while len(terms) > 1:
        half = len(terms) // 2
        terms = [terms[k] + terms[k + half] for k in range(half)]
    return top + jnp.log(terms[0])


def features(coords_ref, rows_ref, wide_ref, left_ref, right_ref):
    tiles = coords_ref.shape[1] // 128
    for d in range(3):
        for t in range(tiles):
            rows_ref[d, t : t + 1, :] = coords_ref[d : d + 1, t * 128 : (t + 1) * 128]
    wide_ref[0 : tiles * 16, :] = jnp.zeros((tiles * 16, 128), F32)
    for at in range(0, tiles, 8):
        x, y, z = (rows_ref[d, at : at + 8, :] for d in range(3))
        norm = x * x + y * y + z * z
        low = norm & 31
        high = norm - low
        one = jnp.ones((8, 128), F32)
        if right_ref is None:
            values = [x, y, z, high, low, one, one]
        else:
            values = [-2 * x, -2 * y, -2 * z, one, one, high, low]
        for k, value in enumerate(values):
            wide_ref[pl.ds(at * 16 + k, 8, stride=16), :] = value.astype(F32)
    if right_ref is None:
        for c in range(tiles // 8):
            left_ref[c] = wide_ref[c * 128 : (c + 1) * 128, :].T.astype(jnp.bfloat16)
    else:
        for t in range(tiles):
            right_ref[t] = wide_ref[t * 16 : (t + 1) * 16, :].astype(jnp.bfloat16)


def squares(sub_coords, lane_coords, sub_ids_ref, lane_ids_ref, rows_ref, wide_ref, left_ref, right_ref, out_ref):
    features(sub_coords, rows_ref, wide_ref, left_ref, None)
    features(lane_coords, rows_ref, wide_ref, None, right_ref)

    def some(g, carry):
        for u in range(GROUP):
            k = g * GROUP + u
            sub = sub_ids_ref[0, 0, k]
            block = right_ref[lane_ids_ref[0, 0, k]]
            member = sub & 7
            right = jnp.concatenate(
                [jnp.where(member == q, block, jnp.zeros_like(block)) for q in range(8)], axis=0
            )
            out_ref[k] = jnp.dot(left_ref[sub >> 3], right, preferred_element_type=F32) * COST
        return carry

    lax.fori_loop(0, SLOTS // GROUP, some, 0)


def half_step(potential, lane_ids_ref, sub_ids_ref, count_ref, square_ref, slots_ref, tops_ref, sums_ref, out_ref):
    sub_tiles = potential.shape[0]
    lane_tiles = tops_ref.shape[0] // 8
    scaled = potential * LOG2E
    if sub_tiles < 128:
        scaled = jnp.concatenate([scaled, jnp.zeros((128 - sub_tiles, 128), jnp.float32)], axis=0)
    columns = scaled.T
    count = count_ref[0, 0]
    places = [pl.ds(pl.multiple_of(lane_ids_ref[0, 0, k] * 8, 8), 8) for k in range(SLOTS)]
    tops_ref[...] = jnp.full(tops_ref.shape, NONE, jnp.float32)
    sums_ref[...] = jnp.zeros(sums_ref.shape, jnp.float32)
    for k in range(SLOTS):
        sub = sub_ids_ref[0, 0, k]
        value = jnp.take_along_axis(columns, jnp.full((128, 128), sub, jnp.int32), axis=1)
        score = (value - square_ref[k]).reshape(16, 8, 128)
        peak = jnp.max(score, axis=0)
        total = jnp.sum(jnp.exp2(score - peak[None]), axis=0)
        slots_ref[k * 8 : k * 8 + 8, :] = jnp.where(k < count, peak * LN2 + jnp.log(total), NONE)
    for k in range(SLOTS):
        tops_ref[places[k], :] = jnp.maximum(tops_ref[places[k], :], slots_ref[k * 8 : k * 8 + 8, :])
    for k in range(SLOTS):
        at = slice(k * 8, k * 8 + 8)
        slots_ref[at, :] = jnp.exp(slots_ref[at, :] - tops_ref[places[k], :])
    for k in range(SLOTS):
        sums_ref[places[k], :] = sums_ref[places[k], :] + slots_ref[k * 8 : k * 8 + 8, :]
    for at in range(0, lane_tiles, 8):
        tops = [tops_ref[pl.ds(at * 8 + q, 8, stride=8), :] for q in range(8)]
        sums = [sums_ref[pl.ds(at * 8 + q, 8, stride=8), :] for q in range(8)]
        top = functools.reduce(jnp.maximum, tops)
        total = functools.reduce(jnp.add, [s * jnp.exp(t - top) for t, s in zip(tops, sums)])
        out_ref[at : at + 8, :] = jnp.where(top > 0.5 * NONE, top + jnp.log(total), NONE)


def put_total(out_ref, mass):
    rows = out_ref.shape[0]
    total = jnp.sum(jnp.sum(mass.astype(F32), axis=0, keepdims=True), axis=1, keepdims=True)
    out_ref[rows - 8 : rows, :] = jnp.broadcast_to(jnp.log(total), (8, 128))


def first_kernel(src_list, tgt_list, count_list, start_in, mass_in, src_in, tgt_in, out, slots, tops, sums, rows, wide, left, right, src_ids, tgt_ids, count, start, mass, src_coords, tgt_coords, square, sems):
    pairs = [(src_list, src_ids), (tgt_list, tgt_ids), (count_list, count), (start_in, start), (mass_in, mass), (src_in, src_coords), (tgt_in, tgt_coords)]
    copies = [pltpu.make_async_copy(here, there, sems.at[n]) for n, (here, there) in enumerate(pairs)]
    for copy in copies:
        copy.start()
    for copy in copies:
        copy.wait()
    squares(tgt_coords, src_coords, tgt_ids, src_ids, rows, wide, left, right, square)
    half_step(start[...], src_ids, tgt_ids, count, square, slots, tops, sums, out)
    put_total(out, mass[...])


def square_kernel(sub_ids, lane_ids, sub_coords, lane_coords, square, rows, wide, left, right):
    squares(sub_coords, lane_coords, sub_ids, lane_ids, rows, wide, left, right, square)


def first_src_kernel(src_ids, tgt_ids, count, m0, m1, m2, m3, src_mass, square, out, tgt_const, slots, tops, sums):
    merged = lse([m0[...], m1[...], m2[...], m3[...]])
    tgt_const[...] = merged[128:136]
    potential = jnp.log(src_mass[...].astype(F32)) - merged[0:128]
    half_step(potential, tgt_ids, src_ids, count, square, slots, tops, sums, out)
    put_total(out, src_mass[...])


def src_kernel(src_ids, tgt_ids, count, m0, m1, m2, m3, src_mass, src_const, square, out, *rest):
    *pot, slots, tops, sums = rest
    potential = jnp.log(src_mass[...].astype(F32)) - src_const[0:1] - lse([m0[...], m1[...], m2[...], m3[...]])
    if pot:
        pot[0][...] = potential
    half_step(potential, tgt_ids, src_ids, count, square, slots, tops, sums, out)


def first_tgt_kernel(src_ids, tgt_ids, count, m0, m1, m2, m3, tgt_mass, tgt_const, square, out, src_const, slots, tops, sums):
    merged = lse([m0[...], m1[...], m2[...], m3[...]])
    src_const[...] = merged[64:72]
    potential = jnp.log(tgt_mass[...].astype(F32)) - tgt_const[0:1] - (merged[0:64] - merged[64:65])
    half_step(potential, src_ids, tgt_ids, count, square, slots, tops, sums, out)


def tgt_kernel(src_ids, tgt_ids, count, m0, m1, m2, m3, tgt_mass, tgt_const, square, out, slots, tops, sums):
    potential = jnp.log(tgt_mass[...].astype(F32)) - tgt_const[0:1] - lse([m0[...], m1[...], m2[...], m3[...]])
    half_step(potential, src_ids, tgt_ids, count, square, slots, tops, sums, out)


SMEM = pl.BlockSpec(memory_space=pltpu.SMEM)
VMEM = pl.BlockSpec(memory_space=pltpu.VMEM)


HBM = pl.BlockSpec(memory_space=pltpu.HBM)
PARAMS = pltpu.CompilerParams(vmem_limit_bytes=12 << 20)
SQUARES = jax.ShapeDtypeStruct((SLOTS, 128, 128), F32)


def half_scratch(lane_tiles):
    return [pltpu.VMEM((SLOTS * 8, 128), F32)] + [pltpu.VMEM((lane_tiles * 8, 128), F32)] * 2


def square_scratch(left_tiles, right_tiles):
    return [
        pltpu.VMEM((3, 128, 128), jnp.int32),
        pltpu.VMEM((2048, 128), F32),
        pltpu.VMEM((left_tiles // 8, 128, 128), jnp.bfloat16),
        pltpu.VMEM((right_tiles, 16, 128), jnp.bfloat16),
    ]


def first_call(*args):
    return pl.pallas_call(
        first_kernel,
        out_shape=jax.ShapeDtypeStruct((136, 128), F32),
        in_specs=[HBM] * 7,
        out_specs=VMEM,
        scratch_shapes=half_scratch(128) + square_scratch(64, 128)
        + [pltpu.SMEM(x.shape, x.dtype) for x in args[:3]]
        + [pltpu.VMEM(x.shape, x.dtype) for x in args[3:]]
        + [pltpu.VMEM(SQUARES.shape, F32), pltpu.SemaphoreType.DMA((7,))],
    )(*args)


def square_call(sub_ids, lane_ids, sub_coords, lane_coords):
    return pl.pallas_call(
        square_kernel, out_shape=SQUARES, in_specs=[SMEM] * 2 + [VMEM] * 2, out_specs=VMEM,
        scratch_shapes=square_scratch(sub_coords.shape[1] // 128, lane_coords.shape[1] // 128), compiler_params=PARAMS,
    )(sub_ids, lane_ids, sub_coords, lane_coords)


def call(body, lane_tiles, outs, *args):
    return pl.pallas_call(
        body,
        out_shape=[jax.ShapeDtypeStruct((rows, 128), F32) for rows in outs],
        in_specs=[SMEM] * 3 + [VMEM] * (len(args) - 3),
        out_specs=[VMEM] * len(outs),
        scratch_shapes=half_scratch(lane_tiles),
        compiler_params=PARAMS,
    )(*args)


def col_permute(value, source):
    pairs = []
    for i in range(32):
        y, z = source(i // 8, i % 8)
        pairs.append((y % 4 * 8 + z % 8, i))
    return lax.ppermute(value, "col", pairs)


def row_permute(value, shift):
    return lax.ppermute(value, "row", [(i, (i + 2 * shift) % 8) for i in range(8)])


def over_col(message):
    merged = lse([
        message,
        col_permute(message, lambda y, z: (y, z ^ 1)),
        col_permute(message, lambda y, z: (y ^ 1, z)),
        col_permute(message, lambda y, z: (y ^ 1, z ^ 1)),
    ])
    merged = lse([merged, col_permute(merged, lambda y, z: (y ^ 3, z))])
    return [merged] + [col_permute(merged, lambda y, z, k=k: (y, z + k if z % 2 else z - k)) for k in (1, 3, -2)]


def over_row(message):
    other = lax.ppermute(message, "row", [(i, i ^ 1) for i in range(8)])
    merged = lse([message, other])
    return [merged] + [row_permute(merged, k) for k in (1, 2, 3)]


def on_device(src_coords, tgt_coords, src_mass, tgt_mass, tgt_start, kept_src, kept_tgt, kept_count):
    src_mass = src_mass.reshape(128, 128)
    tgt_mass = tgt_mass.reshape(64, 128)
    lists = (kept_src, kept_tgt, kept_count)
    message = first_call(*lists, tgt_start.reshape(64, 128), tgt_mass, src_coords, tgt_coords)
    tgt_lanes = square_call(kept_src, kept_tgt, src_coords, tgt_coords)
    src_lanes = square_call(kept_tgt, kept_src, tgt_coords, src_coords)
    for iteration in range(ITERS):
        parts = over_col(message)
        if iteration == 0:
            message, tgt_const = call(first_src_kernel, 64, [72, 8], *lists, *parts, src_mass, tgt_lanes)
        elif iteration + 1 < ITERS:
            (message,) = call(src_kernel, 64, [64], *lists, *parts, src_mass, src_const, tgt_lanes)
        else:
            message, src_potential = call(src_kernel, 64, [64, 128], *lists, *parts, src_mass, src_const, tgt_lanes)
        parts = over_row(message)
        if iteration == 0:
            message, src_const = call(first_tgt_kernel, 128, [128, 8], *lists, *parts, tgt_mass, tgt_const, src_lanes)
        elif iteration + 1 < ITERS:
            (message,) = call(tgt_kernel, 128, [128], *lists, *parts, tgt_mass, tgt_const, src_lanes)
    tgt_potential = jnp.log(tgt_mass.astype(F32)) - tgt_const[0:1] - lse(parts)
    return src_potential.reshape(-1), tgt_potential.reshape(-1)


def solution(mesh):
    placed = (
        P(None, "row"),
        P(None, "col"),
        P("row"),
        P("col"),
        P("col"),
        P("row", "col", None),
        P("row", "col", None),
        P("row", "col"),
    )
    return jax.shard_map(
        on_device, mesh=mesh, in_specs=placed, out_specs=(P("row"), P("col")), check_vma=False
    )
```

profile of v0, /device:TPU:1, one launch (start us, length us, event | category | flops | bytes accessed | tf_op | source)
XLA Modules:
  0.0 123.5 jit_solution(10125789955130680800)
XLA Ops:
  1.3 5.5 %shard_map.95 = f32[136,128]{1,0:T(8,128)} custom-call(s32[1,1,64]{2,1,0:T(1,128)} %src_ids.9, s32[1,1,64]{2,1,0:T(1,128)} %tgt_ids.9, s32[1,1]{1,0:T(1,128)S(6)} %copy.10.count_list.count, f32[64,128]{1,0:T(8,128)} %bitcast.15, s32[64,128]{1,0:T(8,128)} %bitcast.12, s32[3,16384]{1,0:T(4,128)} %lane_coords.3, s32[3,8192]{1,0:T(4,128)} %sub_coords.3), custom_call_target="tpu_custom_call" | custom-call | tf_op jit(solution)/shard_map/pallas_call | solution.py:180
  6.9 2.6 %collective-permute-start = (f32[136,128]{1,0:T(8,128)}, f32[136,128]{1,0:T(8,128)S(1)}, u32[]{:S(2)}, u32[]{:S(2)}) collective-permute-start(f32[136,128]{1,0:T(8,128)} %shard_map.95), channel_id=1, source_target_pairs={{1,0},{0,1},{3,2},{2,3},{5,4},{4,5},{7,6},{6,7},{9,8},{8,9},{11,10... | collective-permute-start | bytes 208904 | tf_op jit(solution)/shard_map/ppermute | solution.py:215
  12.8 2.2 %collective-permute-done.2 = f32[136,128]{1,0:T(8,128)S(1)} collective-permute-done((f32[136,128]{1,0:T(8,128)}, f32[136,128]{1,0:T(8,128)S(1)}, u32[]{:S(2)}, u32[]{:S(2)}) %collective-permute-start.2) | collective-permute-done | bytes 69664 | tf_op jit(solution)/shard_map/ppermute | solution.py:215
  15.9 2.1 %collective-permute-start.3 = (f32[136,128]{1,0:T(8,128)S(1)}, f32[136,128]{1,0:T(8,128)S(1)}, u32[]{:S(2)}, u32[]{:S(2)}) collective-permute-start(f32[136,128]{1,0:T(8,128)S(1)} %log_add_fusion.1), channel_id=1, source_target_pairs={{24,0},{25,1},{26,2},{27,3},{28,4},{29,5},{30,6},{31,7},{16,8},{17... | collective-permute-start | bytes 208904 | tf_op jit(solution)/shard_map/ppermute | solution.py:215
  18.0 2.4 %collective-permute-done.3 = f32[136,128]{1,0:T(8,128)S(1)} collective-permute-done((f32[136,128]{1,0:T(8,128)S(1)}, f32[136,128]{1,0:T(8,128)S(1)}, u32[]{:S(2)}, u32[]{:S(2)}) %collective-permute-start.3) | collective-permute-done | bytes 69664 | tf_op jit(solution)/shard_map/ppermute | solution.py:215
  20.4 4.7 %collective-permute-start.4 = (f32[136,128]{1,0:T(8,128)S(1)}, f32[136,128]{1,0:T(8,128)S(1)}, u32[]{:S(2)}, u32[]{:S(2)}) collective-permute-start(f32[136,128]{1,0:T(8,128)S(1)} %log_add_fusion.m0), channel_id=1, source_target_pairs={{7,0},{2,1},{1,2},{4,3},{3,4},{6,5},{5,6},{0,7},{15,8},{10,9},{9,1... | collective-permute-start | bytes 208904 | tf_op jit(solution)/shard_map/ppermute | solution.py:215
  26.8 2.4 %collective-permute-start.6 = (f32[136,128]{1,0:T(8,128)S(1)}, f32[136,128]{1,0:T(8,128)S(1)}, u32[]{:S(2)}, u32[]{:S(2)}) collective-permute-start(f32[136,128]{1,0:T(8,128)S(1)} %log_add_fusion.m0), channel_id=1, source_target_pairs={{2,0},{7,1},{4,2},{1,3},{6,4},{3,5},{0,6},{5,7},{10,8},{15,9},{12,... | collective-permute-start | bytes 208904 | tf_op jit(solution)/shard_map/ppermute | solution.py:215
  32.4 2.4 %shard_map.96.square = f32[64,128,128]{2,1,0:T(8,128)S(1)} custom-call(s32[1,1,64]{2,1,0:T(1,128)S(1)} %copy-done.4, s32[1,1,64]{2,1,0:T(1,128)S(1)} %copy-done.5, s32[3,16384]{1,0:T(4,128)S(1)} %copy-done, s32[3,8192]{1,0:T(4,128)S(1)} %copy-done.1), custom_call_target="tpu_custom_call" | custom-call | tf_op jit(solution)/shard_map/pallas_call | solution.py:193
  34.8 2.6 %shard_map.97 = (f32[72,128]{1,0:T(8,128)S(1)}, f32[8,128]{1,0:T(8,128)S(1)}) custom-call(s32[1,1,64]{2,1,0:T(1,128)S(1)} %copy-done.4, s32[1,1,64]{2,1,0:T(1,128)S(1)} %copy-done.5, s32[1,1]{1,0:T(1,128)S(6)} %copy.10.count_list.count, f32[136,128]{1,0:T(8,128)S(1)} %log_add_fusion.m0, f32[136,128]{1,0:T(8,128)S(1)} %collective-permute-done.4.m1, ...), custom_call_target="tpu_custom_call" | custom-call | tf_op jit(solution)/shard_map/pallas_call | solution.py:200
  37.5 4.5 %collective-permute-start.7 = (f32[72,128]{1,0:T(8,128)S(1)}, f32[72,128]{1,0:T(8,128)S(1)}, u32[]{:S(2)}, u32[]{:S(2)}) collective-permute-start(f32[72,128]{1,0:T(8,128)S(1)} %get-tuple-element.8), channel_id=1, source_target_pairs={{0,32},{32,0},{64,96},{96,64},{128,160},{160,128},{192,224},{224,1... | collective-permute-start | bytes 110600 | tf_op jit(solution)/shard_map/ppermute | solution.py:234
  42.8 2.6 %collective-permute-start.10 = (f32[72,128]{1,0:T(8,128)S(1)}, f32[72,128]{1,0:T(8,128)S(1)}, u32[]{:S(2)}, u32[]{:S(2)}) collective-permute-start(f32[72,128]{1,0:T(8,128)S(1)} %log_add_fusion.6.m0), channel_id=1, source_target_pairs={{0,192},{32,224},{64,0},{96,32},{128,64},{160,96},{192,128},{224,1... | collective-permute-start | bytes 110600 | tf_op jit(solution)/shard_map/ppermute | solution.py:219
  45.4 1.7 %collective-permute-start.9 = (f32[72,128]{1,0:T(8,128)S(1)}, f32[72,128]{1,0:T(8,128)S(1)}, u32[]{:S(2)}, u32[]{:S(2)}) collective-permute-start(f32[72,128]{1,0:T(8,128)S(1)} %log_add_fusion.6.m0), channel_id=1, source_target_pairs={{0,128},{32,160},{64,192},{96,224},{128,0},{160,32},{192,64},{224,... | collective-permute-start | bytes 110600 | tf_op jit(solution)/shard_map/ppermute | solution.py:219
  47.1 2.3 %shard_map.98.square = f32[64,128,128]{2,1,0:T(8,128)S(1)} custom-call(s32[1,1,64]{2,1,0:T(1,128)S(1)} %copy-done.5, s32[1,1,64]{2,1,0:T(1,128)S(1)} %copy-done.4, s32[3,8192]{1,0:T(4,128)S(1)} %copy-done.1, s32[3,16384]{1,0:T(4,128)S(1)} %copy-done), custom_call_target="tpu_custom_call" | custom-call | tf_op jit(solution)/shard_map/pallas_call | solution.py:193
  50.0 2.7 %shard_map.99 = (f32[128,128]{1,0:T(8,128)S(1)}, f32[8,128]{1,0:T(8,128)S(1)}) custom-call(s32[1,1,64]{2,1,0:T(1,128)S(1)} %copy-done.4, s32[1,1,64]{2,1,0:T(1,128)S(1)} %copy-done.5, s32[1,1]{1,0:T(1,128)S(6)} %copy.10.count_list.count, f32[72,128]{1,0:T(8,128)S(1)} %log_add_fusion.6.m0, f32[72,128]{1,0:T(8,128)S(1)} %collective-permute-done.8.m1, ...), custom_call_target="tpu_custom_call" | custom-call | tf_op jit(solution)/shard_map/pallas_call | solution.py:200
  52.9 2.5 %collective-permute-start.13 = (f32[128,128]{1,0:T(8,128)S(1)}, f32[128,128]{1,0:T(8,128)S(1)}, u32[]{:S(2)}, u32[]{:S(2)}) collective-permute-start(f32[128,128]{1,0:T(8,128)S(1)} %get-tuple-element.10), channel_id=1, source_target_pairs={{9,0},{8,1},{11,2},{10,3},{13,4},{12,5},{15,6},{14,7},{1,8},{0,9},... | collective-permute-start | bytes 196616 | tf_op jit(solution)/shard_map/ppermute | solution.py:215
  56.0 1.8 %collective-permute-done.13 = f32[128,128]{1,0:T(8,128)S(1)} collective-permute-done((f32[128,128]{1,0:T(8,128)S(1)}, f32[128,128]{1,0:T(8,128)S(1)}, u32[]{:S(2)}, u32[]{:S(2)}) %collective-permute-start.13) | collective-permute-done | bytes 65568 | tf_op jit(solution)/shard_map/ppermute | solution.py:215
  59.5 2.8 %collective-permute-done.14 = f32[128,128]{1,0:T(8,128)S(1)} collective-permute-done((f32[128,128]{1,0:T(8,128)S(1)}, f32[128,128]{1,0:T(8,128)S(1)}, u32[]{:S(2)}, u32[]{:S(2)}) %collective-permute-start.14) | collective-permute-done | bytes 65568 | tf_op jit(solution)/shard_map/ppermute | solution.py:215
  64.0 2.5 %collective-permute-start.17 = (f32[128,128]{1,0:T(8,128)S(1)}, f32[128,128]{1,0:T(8,128)S(1)}, u32[]{:S(2)}, u32[]{:S(2)}) collective-permute-start(f32[128,128]{1,0:T(8,128)S(1)} %log_add_fusion.4.m0), channel_id=1, source_target_pairs={{2,0},{7,1},{4,2},{1,3},{6,4},{3,5},{0,6},{5,7},{10,8},{15,9},{12,... | collective-permute-start | bytes 196616 | tf_op jit(solution)/shard_map/ppermute | solution.py:215
  66.8 2.0 %collective-permute-done.16.m2 = f32[128,128]{1,0:T(8,128)S(1)} collective-permute-done((f32[128,128]{1,0:T(8,128)S(1)}, f32[128,128]{1,0:T(8,128)S(1)}, u32[]{:S(2)}, u32[]{:S(2)}) %collective-permute-start.16) | collective-permute-done | bytes 65568 | tf_op jit(solution)/shard_map/ppermute | solution.py:215
  68.8 2.3 %collective-permute-done.17.m3 = f32[128,128]{1,0:T(8,128)S(1)} collective-permute-done((f32[128,128]{1,0:T(8,128)S(1)}, f32[128,128]{1,0:T(8,128)S(1)}, u32[]{:S(2)}, u32[]{:S(2)}) %collective-permute-start.17) | collective-permute-done | bytes 65568 | tf_op jit(solution)/shard_map/ppermute | solution.py:215
  71.1 2.6 %shard_map.100 = f32[64,128]{1,0:T(8,128)S(1)} custom-call(s32[1,1,64]{2,1,0:T(1,128)S(1)} %copy-done.4, s32[1,1,64]{2,1,0:T(1,128)S(1)} %copy-done.5, s32[1,1]{1,0:T(1,128)S(6)} %copy.10.count_list.count, f32[128,128]{1,0:T(8,128)S(1)} %log_add_fusion.4.m0, f32[128,128]{1,0:T(8,128)S(1)} %collective-permute-done.15.m1, ...), custom_call_target="tpu_custom_call" | custom-call | tf_op jit(solution)/shard_map/pallas_call | solution.py:200
  73.7 3.5 %collective-permute-start.18 = (f32[64,128]{1,0:T(8,128)S(1)}, f32[64,128]{1,0:T(8,128)S(1)}, u32[]{:S(2)}, u32[]{:S(2)}) collective-permute-start(f32[64,128]{1,0:T(8,128)S(1)} %shard_map.100), channel_id=1, source_target_pairs={{0,32},{32,0},{64,96},{96,64},{128,160},{160,128},{192,224},{224,1... | collective-permute-start | bytes 98312 | tf_op jit(solution)/shard_map/ppermute | solution.py:234
  78.7 3.4 %collective-permute-start.20 = (f32[64,128]{1,0:T(8,128)S(1)}, f32[64,128]{1,0:T(8,128)S(1)}, u32[]{:S(2)}, u32[]{:S(2)}) collective-permute-start(f32[64,128]{1,0:T(8,128)S(1)} %log_add_fusion.8.m0), channel_id=1, source_target_pairs={{0,128},{32,160},{64,192},{96,224},{128,0},{160,32},{192,64},{224,... | collective-permute-start | bytes 98312 | tf_op jit(solution)/shard_map/ppermute | solution.py:219
  84.9 2.7 %shard_map.101 = f32[128,128]{1,0:T(8,128)S(1)} custom-call(s32[1,1,64]{2,1,0:T(1,128)S(1)} %copy-done.4, s32[1,1,64]{2,1,0:T(1,128)S(1)} %copy-done.5, s32[1,1]{1,0:T(1,128)S(6)} %copy.10.count_list.count, f32[64,128]{1,0:T(8,128)S(1)} %log_add_fusion.8.m0, f32[64,128]{1,0:T(8,128)S(1)} %collective-permute-done.19.m1, ...), custom_call_target="tpu_custom_call" | custom-call | tf_op jit(solution)/shard_map/pallas_call | solution.py:200
  87.6 2.8 %collective-permute-start.22 = (f32[128,128]{1,0:T(8,128)S(1)}, f32[128,128]{1,0:T(8,128)S(1)}, u32[]{:S(2)}, u32[]{:S(2)}) collective-permute-start(f32[128,128]{1,0:T(8,128)S(1)} %shard_map.101), channel_id=1, source_target_pairs={{1,0},{0,1},{3,2},{2,3},{5,4},{4,5},{7,6},{6,7},{9,8},{8,9},{11,10... | collective-permute-start | bytes 196616 | tf_op jit(solution)/shard_map/ppermute | solution.py:215
  94.8 2.0 %collective-permute-start.25 = (f32[128,128]{1,0:T(8,128)S(1)}, f32[128,128]{1,0:T(8,128)S(1)}, u32[]{:S(2)}, u32[]{:S(2)}) collective-permute-start(f32[128,128]{1,0:T(8,128)S(1)} %log_add_fusion.3), channel_id=1, source_target_pairs={{24,0},{25,1},{26,2},{27,3},{28,4},{29,5},{30,6},{31,7},{16,8},{17... | collective-permute-start | bytes 196616 | tf_op jit(solution)/shard_map/ppermute | solution.py:215
  96.8 2.4 %collective-permute-done.25 = f32[128,128]{1,0:T(8,128)S(1)} collective-permute-done((f32[128,128]{1,0:T(8,128)S(1)}, f32[128,128]{1,0:T(8,128)S(1)}, u32[]{:S(2)}, u32[]{:S(2)}) %collective-permute-start.25) | collective-permute-done | bytes 65568 | tf_op jit(solution)/shard_map/ppermute | solution.py:215
  101.2 3.5 %collective-permute-start.28 = (f32[128,128]{1,0:T(8,128)S(1)}, f32[128,128]{1,0:T(8,128)S(1)}, u32[]{:S(2)}, u32[]{:S(2)}) collective-permute-start(f32[128,128]{1,0:T(8,128)S(1)} %log_add_fusion.2.m0), channel_id=1, source_target_pairs={{2,0},{7,1},{4,2},{1,3},{6,4},{3,5},{0,6},{5,7},{10,8},{15,9},{12,... | collective-permute-start | bytes 196616 | tf_op jit(solution)/shard_map/ppermute | solution.py:215
  104.7 2.8 %collective-permute-done.27.m2 = f32[128,128]{1,0:T(8,128)S(1)} collective-permute-done((f32[128,128]{1,0:T(8,128)S(1)}, f32[128,128]{1,0:T(8,128)S(1)}, u32[]{:S(2)}, u32[]{:S(2)}) %collective-permute-start.27) | collective-permute-done | bytes 65568 | tf_op jit(solution)/shard_map/ppermute | solution.py:215
  107.8 3.2 %shard_map.102 = (f32[64,128]{1,0:T(8,128)S(1)}, f32[128,128]{1,0:T(8,128)}) custom-call(s32[1,1,64]{2,1,0:T(1,128)S(1)} %copy-done.4, s32[1,1,64]{2,1,0:T(1,128)S(1)} %copy-done.5, s32[1,1]{1,0:T(1,128)S(6)} %copy.10.count_list.count, f32[128,128]{1,0:T(8,128)S(1)} %log_add_fusion.2.m0, f32[128,128]{1,0:T(8,128)S(1)} %collective-permute-done.26.m1, ...), custom_call_target="tpu_custom_call" | custom-call | tf_op jit(solution)/shard_map/pallas_call | solution.py:200
  111.0 5.5 %collective-permute-start.29 = (f32[64,128]{1,0:T(8,128)S(1)}, f32[64,128]{1,0:T(8,128)S(1)}, u32[]{:S(2)}, u32[]{:S(2)}) collective-permute-start(f32[64,128]{1,0:T(8,128)S(1)} %get-tuple-element.13), channel_id=1, source_target_pairs={{0,32},{32,0},{64,96},{96,64},{128,160},{160,128},{192,224},{224,1... | collective-permute-start | bytes 98312 | tf_op jit(solution)/shard_map/ppermute | solution.py:234
  117.4 2.3 %collective-permute-start.31 = (f32[64,128]{1,0:T(8,128)S(1)}, f32[64,128]{1,0:T(8,128)S(1)}, u32[]{:S(2)}, u32[]{:S(2)}) collective-permute-start(f32[64,128]{1,0:T(8,128)S(1)} %log_add_fusion.7), channel_id=1, source_target_pairs={{0,128},{32,160},{64,192},{96,224},{128,0},{160,32},{192,64},{224,... | collective-permute-start | bytes 98312 | tf_op jit(solution)/shard_map/ppermute | solution.py:219
  (65 shorter events, 30.6 us)
Async XLA Ops:
  6.9 4.5 %collective-permute-start = (f32[136,128]{1,0:T(8,128)}, f32[136,128]{1,0:T(8,128)S(1)}, u32[]{:S(2)}, u32[]{:S(2)}) collective-permute-start(f32[136,128]{1,0:T(8,128)} %shard_map.95), channel_id=1, source_target_pairs={{1,0},{0,1},{3,2},{2,3},{5,4},{4,5},{7,6},{6,7},{9,8},{8,9},{11,10... | collective-permute-start | bytes 208904 | tf_op jit(solution)/shard_map/ppermute | solution.py:215
  9.4 3.4 %collective-permute-start.1 = (f32[136,128]{1,0:T(8,128)}, f32[136,128]{1,0:T(8,128)S(1)}, u32[]{:S(2)}, u32[]{:S(2)}) collective-permute-start(f32[136,128]{1,0:T(8,128)} %shard_map.95), channel_id=1, source_target_pairs={{8,0},{9,1},{10,2},{11,3},{12,4},{13,5},{14,6},{15,7},{0,8},{1,9},... | collective-permute-start | bytes 208904 | tf_op jit(solution)/shard_map/ppermute | solution.py:215
  10.7 4.3 %collective-permute-start.2 = (f32[136,128]{1,0:T(8,128)}, f32[136,128]{1,0:T(8,128)S(1)}, u32[]{:S(2)}, u32[]{:S(2)}) collective-permute-start(f32[136,128]{1,0:T(8,128)} %shard_map.95), channel_id=1, source_target_pairs={{9,0},{8,1},{11,2},{10,3},{13,4},{12,5},{15,6},{14,7},{1,8},{0,9},... | collective-permute-start | bytes 208904 | tf_op jit(solution)/shard_map/ppermute | solution.py:215
  15.9 4.5 %collective-permute-start.3 = (f32[136,128]{1,0:T(8,128)S(1)}, f32[136,128]{1,0:T(8,128)S(1)}, u32[]{:S(2)}, u32[]{:S(2)}) collective-permute-start(f32[136,128]{1,0:T(8,128)S(1)} %log_add_fusion.1), channel_id=1, source_target_pairs={{24,0},{25,1},{26,2},{27,3},{28,4},{29,5},{30,6},{31,7},{16,8},{17... | collective-permute-start | bytes 208904 | tf_op jit(solution)/shard_map/ppermute | solution.py:215
  20.4 14.3 %collective-permute-start.4 = (f32[136,128]{1,0:T(8,128)S(1)}, f32[136,128]{1,0:T(8,128)S(1)}, u32[]{:S(2)}, u32[]{:S(2)}) collective-permute-start(f32[136,128]{1,0:T(8,128)S(1)} %log_add_fusion.m0), channel_id=1, source_target_pairs={{7,0},{2,1},{1,2},{4,3},{3,4},{6,5},{5,6},{0,7},{15,8},{10,9},{9,1... | collective-permute-start | bytes 208904 | tf_op jit(solution)/shard_map/ppermute | solution.py:215
  25.2 9.6 %collective-permute-start.5 = (f32[136,128]{1,0:T(8,128)S(1)}, f32[136,128]{1,0:T(8,128)S(1)}, u32[]{:S(2)}, u32[]{:S(2)}) collective-permute-start(f32[136,128]{1,0:T(8,128)S(1)} %log_add_fusion.m0), channel_id=1, source_target_pairs={{5,0},{4,1},{7,2},{6,3},{1,4},{0,5},{3,6},{2,7},{13,8},{12,9},{15,... | collective-permute-start | bytes 208904 | tf_op jit(solution)/shard_map/ppermute | solution.py:215
  26.8 8.0 %collective-permute-start.6 = (f32[136,128]{1,0:T(8,128)S(1)}, f32[136,128]{1,0:T(8,128)S(1)}, u32[]{:S(2)}, u32[]{:S(2)}) collective-permute-start(f32[136,128]{1,0:T(8,128)S(1)} %log_add_fusion.m0), channel_id=1, source_target_pairs={{2,0},{7,1},{4,2},{1,3},{6,4},{3,5},{0,6},{5,7},{10,8},{15,9},{12,... | collective-permute-start | bytes 208904 | tf_op jit(solution)/shard_map/ppermute | solution.py:215
  37.5 5.3 %collective-permute-start.7 = (f32[72,128]{1,0:T(8,128)S(1)}, f32[72,128]{1,0:T(8,128)S(1)}, u32[]{:S(2)}, u32[]{:S(2)}) collective-permute-start(f32[72,128]{1,0:T(8,128)S(1)} %get-tuple-element.8), channel_id=1, source_target_pairs={{0,32},{32,0},{64,96},{96,64},{128,160},{160,128},{192,224},{224,1... | collective-permute-start | bytes 110600 | tf_op jit(solution)/shard_map/ppermute | solution.py:234
  42.8 6.6 %collective-permute-start.10 = (f32[72,128]{1,0:T(8,128)S(1)}, f32[72,128]{1,0:T(8,128)S(1)}, u32[]{:S(2)}, u32[]{:S(2)}) collective-permute-start(f32[72,128]{1,0:T(8,128)S(1)} %log_add_fusion.6.m0), channel_id=1, source_target_pairs={{0,192},{32,224},{64,0},{96,32},{128,64},{160,96},{192,128},{224,1... | collective-permute-start | bytes 110600 | tf_op jit(solution)/shard_map/ppermute | solution.py:219
  45.4 4.1 %collective-permute-start.8 = (f32[72,128]{1,0:T(8,128)S(1)}, f32[72,128]{1,0:T(8,128)S(1)}, u32[]{:S(2)}, u32[]{:S(2)}) collective-permute-start(f32[72,128]{1,0:T(8,128)S(1)} %log_add_fusion.6.m0), channel_id=1, source_target_pairs={{0,64},{32,96},{64,128},{96,160},{128,192},{160,224},{192,0},{224,... | collective-permute-start | bytes 110600 | tf_op jit(solution)/shard_map/ppermute | solution.py:219
  45.4 4.6 %collective-permute-start.9 = (f32[72,128]{1,0:T(8,128)S(1)}, f32[72,128]{1,0:T(8,128)S(1)}, u32[]{:S(2)}, u32[]{:S(2)}) collective-permute-start(f32[72,128]{1,0:T(8,128)S(1)} %log_add_fusion.6.m0), channel_id=1, source_target_pairs={{0,128},{32,160},{64,192},{96,224},{128,0},{160,32},{192,64},{224,... | collective-permute-start | bytes 110600 | tf_op jit(solution)/shard_map/ppermute | solution.py:219
  52.7 3.2 %collective-permute-start.11 = (f32[128,128]{1,0:T(8,128)S(1)}, f32[128,128]{1,0:T(8,128)S(1)}, u32[]{:S(2)}, u32[]{:S(2)}) collective-permute-start(f32[128,128]{1,0:T(8,128)S(1)} %get-tuple-element.10), channel_id=1, source_target_pairs={{1,0},{0,1},{3,2},{2,3},{5,4},{4,5},{7,6},{6,7},{9,8},{8,9},{11,10... | collective-permute-start | bytes 196616 | tf_op jit(solution)/shard_map/ppermute | solution.py:215
  52.8 3.2 %collective-permute-start.12 = (f32[128,128]{1,0:T(8,128)S(1)}, f32[128,128]{1,0:T(8,128)S(1)}, u32[]{:S(2)}, u32[]{:S(2)}) collective-permute-start(f32[128,128]{1,0:T(8,128)S(1)} %get-tuple-element.10), channel_id=1, source_target_pairs={{8,0},{9,1},{10,2},{11,3},{12,4},{13,5},{14,6},{15,7},{0,8},{1,9},... | collective-permute-start | bytes 196616 | tf_op jit(solution)/shard_map/ppermute | solution.py:215
  52.9 5.0 %collective-permute-start.13 = (f32[128,128]{1,0:T(8,128)S(1)}, f32[128,128]{1,0:T(8,128)S(1)}, u32[]{:S(2)}, u32[]{:S(2)}) collective-permute-start(f32[128,128]{1,0:T(8,128)S(1)} %get-tuple-element.10), channel_id=1, source_target_pairs={{9,0},{8,1},{11,2},{10,3},{13,4},{12,5},{15,6},{14,7},{1,8},{0,9},... | collective-permute-start | bytes 196616 | tf_op jit(solution)/shard_map/ppermute | solution.py:215
  57.9 4.4 %collective-permute-start.14 = (f32[128,128]{1,0:T(8,128)S(1)}, f32[128,128]{1,0:T(8,128)S(1)}, u32[]{:S(2)}, u32[]{:S(2)}) collective-permute-start(f32[128,128]{1,0:T(8,128)S(1)} %log_add_fusion.5), channel_id=1, source_target_pairs={{24,0},{25,1},{26,2},{27,3},{28,4},{29,5},{30,6},{31,7},{16,8},{17... | collective-permute-start | bytes 196616 | tf_op jit(solution)/shard_map/ppermute | solution.py:215
  62.4 4.4 %collective-permute-start.15 = (f32[128,128]{1,0:T(8,128)S(1)}, f32[128,128]{1,0:T(8,128)S(1)}, u32[]{:S(2)}, u32[]{:S(2)}) collective-permute-start(f32[128,128]{1,0:T(8,128)S(1)} %log_add_fusion.4.m0), channel_id=1, source_target_pairs={{7,0},{2,1},{1,2},{4,3},{3,4},{6,5},{5,6},{0,7},{15,8},{10,9},{9,1... | collective-permute-start | bytes 196616 | tf_op jit(solution)/shard_map/ppermute | solution.py:215
  62.5 6.3 %collective-permute-start.16 = (f32[128,128]{1,0:T(8,128)S(1)}, f32[128,128]{1,0:T(8,128)S(1)}, u32[]{:S(2)}, u32[]{:S(2)}) collective-permute-start(f32[128,128]{1,0:T(8,128)S(1)} %log_add_fusion.4.m0), channel_id=1, source_target_pairs={{5,0},{4,1},{7,2},{6,3},{1,4},{0,5},{3,6},{2,7},{13,8},{12,9},{15,... | collective-permute-start | bytes 196616 | tf_op jit(solution)/shard_map/ppermute | solution.py:215
  64.0 7.0 %collective-permute-start.17 = (f32[128,128]{1,0:T(8,128)S(1)}, f32[128,128]{1,0:T(8,128)S(1)}, u32[]{:S(2)}, u32[]{:S(2)}) collective-permute-start(f32[128,128]{1,0:T(8,128)S(1)} %log_add_fusion.4.m0), channel_id=1, source_target_pairs={{2,0},{7,1},{4,2},{1,3},{6,4},{3,5},{0,6},{5,7},{10,8},{15,9},{12,... | collective-permute-start | bytes 196616 | tf_op jit(solution)/shard_map/ppermute | solution.py:215
  73.7 4.3 %collective-permute-start.18 = (f32[64,128]{1,0:T(8,128)S(1)}, f32[64,128]{1,0:T(8,128)S(1)}, u32[]{:S(2)}, u32[]{:S(2)}) collective-permute-start(f32[64,128]{1,0:T(8,128)S(1)} %shard_map.100), channel_id=1, source_target_pairs={{0,32},{32,0},{64,96},{96,64},{128,160},{160,128},{192,224},{224,1... | collective-permute-start | bytes 98312 | tf_op jit(solution)/shard_map/ppermute | solution.py:234
  78.0 4.2 %collective-permute-start.19 = (f32[64,128]{1,0:T(8,128)S(1)}, f32[64,128]{1,0:T(8,128)S(1)}, u32[]{:S(2)}, u32[]{:S(2)}) collective-permute-start(f32[64,128]{1,0:T(8,128)S(1)} %log_add_fusion.8.m0), channel_id=1, source_target_pairs={{0,64},{32,96},{64,128},{96,160},{128,192},{160,224},{192,0},{224,... | collective-permute-start | bytes 98312 | tf_op jit(solution)/shard_map/ppermute | solution.py:219
  78.7 5.1 %collective-permute-start.20 = (f32[64,128]{1,0:T(8,128)S(1)}, f32[64,128]{1,0:T(8,128)S(1)}, u32[]{:S(2)}, u32[]{:S(2)}) collective-permute-start(f32[64,128]{1,0:T(8,128)S(1)} %log_add_fusion.8.m0), channel_id=1, source_target_pairs={{0,128},{32,160},{64,192},{96,224},{128,0},{160,32},{192,64},{224,... | collective-permute-start | bytes 98312 | tf_op jit(solution)/shard_map/ppermute | solution.py:219
  87.6 4.4 %collective-permute-start.22 = (f32[128,128]{1,0:T(8,128)S(1)}, f32[128,128]{1,0:T(8,128)S(1)}, u32[]{:S(2)}, u32[]{:S(2)}) collective-permute-start(f32[128,128]{1,0:T(8,128)S(1)} %shard_map.101), channel_id=1, source_target_pairs={{1,0},{0,1},{3,2},{2,3},{5,4},{4,5},{7,6},{6,7},{9,8},{8,9},{11,10... | collective-permute-start | bytes 196616 | tf_op jit(solution)/shard_map/ppermute | solution.py:215
  90.4 3.1 %collective-permute-start.23 = (f32[128,128]{1,0:T(8,128)S(1)}, f32[128,128]{1,0:T(8,128)S(1)}, u32[]{:S(2)}, u32[]{:S(2)}) collective-permute-start(f32[128,128]{1,0:T(8,128)S(1)} %shard_map.101), channel_id=1, source_target_pairs={{8,0},{9,1},{10,2},{11,3},{12,4},{13,5},{14,6},{15,7},{0,8},{1,9},... | collective-permute-start | bytes 196616 | tf_op jit(solution)/shard_map/ppermute | solution.py:215
  90.5 4.3 %collective-permute-start.24 = (f32[128,128]{1,0:T(8,128)S(1)}, f32[128,128]{1,0:T(8,128)S(1)}, u32[]{:S(2)}, u32[]{:S(2)}) collective-permute-start(f32[128,128]{1,0:T(8,128)S(1)} %shard_map.101), channel_id=1, source_target_pairs={{9,0},{8,1},{11,2},{10,3},{13,4},{12,5},{15,6},{14,7},{1,8},{0,9},... | collective-permute-start | bytes 196616 | tf_op jit(solution)/shard_map/ppermute | solution.py:215
  94.8 4.4 %collective-permute-start.25 = (f32[128,128]{1,0:T(8,128)S(1)}, f32[128,128]{1,0:T(8,128)S(1)}, u32[]{:S(2)}, u32[]{:S(2)}) collective-permute-start(f32[128,128]{1,0:T(8,128)S(1)} %log_add_fusion.3), channel_id=1, source_target_pairs={{24,0},{25,1},{26,2},{27,3},{28,4},{29,5},{30,6},{31,7},{16,8},{17... | collective-permute-start | bytes 196616 | tf_op jit(solution)/shard_map/ppermute | solution.py:215
  99.3 5.4 %collective-permute-start.26 = (f32[128,128]{1,0:T(8,128)S(1)}, f32[128,128]{1,0:T(8,128)S(1)}, u32[]{:S(2)}, u32[]{:S(2)}) collective-permute-start(f32[128,128]{1,0:T(8,128)S(1)} %log_add_fusion.2.m0), channel_id=1, source_target_pairs={{7,0},{2,1},{1,2},{4,3},{3,4},{6,5},{5,6},{0,7},{15,8},{10,9},{9,1... | collective-permute-start | bytes 196616 | tf_op jit(solution)/shard_map/ppermute | solution.py:215
  100.7 6.8 %collective-permute-start.27 = (f32[128,128]{1,0:T(8,128)S(1)}, f32[128,128]{1,0:T(8,128)S(1)}, u32[]{:S(2)}, u32[]{:S(2)}) collective-permute-start(f32[128,128]{1,0:T(8,128)S(1)} %log_add_fusion.2.m0), channel_id=1, source_target_pairs={{5,0},{4,1},{7,2},{6,3},{1,4},{0,5},{3,6},{2,7},{13,8},{12,9},{15,... | collective-permute-start | bytes 196616 | tf_op jit(solution)/shard_map/ppermute | solution.py:215
  101.2 6.6 %collective-permute-start.28 = (f32[128,128]{1,0:T(8,128)S(1)}, f32[128,128]{1,0:T(8,128)S(1)}, u32[]{:S(2)}, u32[]{:S(2)}) collective-permute-start(f32[128,128]{1,0:T(8,128)S(1)} %log_add_fusion.2.m0), channel_id=1, source_target_pairs={{2,0},{7,1},{4,2},{1,3},{6,4},{3,5},{0,6},{5,7},{10,8},{15,9},{12,... | collective-permute-start | bytes 196616 | tf_op jit(solution)/shard_map/ppermute | solution.py:215
  111.0 6.3 %collective-permute-start.29 = (f32[64,128]{1,0:T(8,128)S(1)}, f32[64,128]{1,0:T(8,128)S(1)}, u32[]{:S(2)}, u32[]{:S(2)}) collective-permute-start(f32[64,128]{1,0:T(8,128)S(1)} %get-tuple-element.13), channel_id=1, source_target_pairs={{0,32},{32,0},{64,96},{96,64},{128,160},{160,128},{192,224},{224,1... | collective-permute-start | bytes 98312 | tf_op jit(solution)/shard_map/ppermute | solution.py:234
  117.3 4.1 %collective-permute-start.30 = (f32[64,128]{1,0:T(8,128)S(1)}, f32[64,128]{1,0:T(8,128)S(1)}, u32[]{:S(2)}, u32[]{:S(2)}) collective-permute-start(f32[64,128]{1,0:T(8,128)S(1)} %log_add_fusion.7), channel_id=1, source_target_pairs={{0,64},{32,96},{64,128},{96,160},{128,192},{160,224},{192,0},{224,... | collective-permute-start | bytes 98312 | tf_op jit(solution)/shard_map/ppermute | solution.py:219
  117.4 4.6 %collective-permute-start.31 = (f32[64,128]{1,0:T(8,128)S(1)}, f32[64,128]{1,0:T(8,128)S(1)}, u32[]{:S(2)}, u32[]{:S(2)}) collective-permute-start(f32[64,128]{1,0:T(8,128)S(1)} %log_add_fusion.7), channel_id=1, source_target_pairs={{0,128},{32,160},{64,192},{96,224},{128,0},{160,32},{192,64},{224,... | collective-permute-start | bytes 98312 | tf_op jit(solution)/shard_map/ppermute | solution.py:219
  119.7 3.1 %collective-permute-start.32 = (f32[64,128]{1,0:T(8,128)S(1)}, f32[64,128]{1,0:T(8,128)S(1)}, u32[]{:S(2)}, u32[]{:S(2)}) collective-permute-start(f32[64,128]{1,0:T(8,128)S(1)} %log_add_fusion.7), channel_id=1, source_target_pairs={{0,192},{32,224},{64,0},{96,32},{128,64},{160,96},{192,128},{224,1... | collective-permute-start | bytes 98312 | tf_op jit(solution)/shard_map/ppermute | solution.py:219
  (7 other events, 55.2 us)
where the time goes:
time: 124 us; the launch traced here: 123 us
  starting transfers between devices  59.8 us (48%)
  waiting for transfers between devices  32.9 us (27%)
  Pallas kernels  24.1 us (19%)
  local copies, waits for them, and re-layouts  3.17 us (3%)
  other arithmetic  1.96 us (2%)
  between operations  1.49 us (1%)
    ppermute x21, starting transfers between devices, col_permute(): return lax.ppermute(value, 'col', pairs)  34.7 us
    ppermute x21, waiting for transfers between devices, col_permute(): return lax.ppermute(value, 'col', pairs)  25 us
    pallas_call x5, Pallas kernels, call(): pl.pallas_call(body, out_shape=[jax.ShapeDtypeStruct((rows, 128), F32) fo...  13.8 us
    ppermute x3, starting transfers between devices, over_row(): other = lax.ppermute(message, 'row', [(i, i ^ 1) for i in range(8)])  13.4 us
    ppermute x9, starting transfers between devices, row_permute(): lax.ppermute(value, 'row', [(i, (i + 2 * shift) % 8) for i in range(8)])  11.8 us
    pallas_call x1, Pallas kernels, first_call(): pl.pallas_call(first_kernel, out_shape=jax.ShapeDtypeStruct((136, 128), F...  5.53 us
    ppermute x9, waiting for transfers between devices, row_permute(): lax.ppermute(value, 'row', [(i, (i + 2 * shift) % 8) for i in range(8)])  5.37 us
    pallas_call x2, Pallas kernels, square_call(): pl.pallas_call(square_kernel, out_shape=SQUARES, in_specs=[SMEM] * 2 + [V...  4.69 us
  transfers between devices with their start and end apart: 33, of which 28 were waited for; matrix products, arithmetic and copies ran while one was open for 0% of the time, Pallas kernels for 4%

commit v1 on v0

--- a/solution.py
+++ b/solution.py
@@ -71,20 +71,24 @@
     lax.fori_loop(0, SLOTS // GROUP, some, 0)
 
 
-def half_step(potential, lane_ids_ref, sub_ids_ref, count_ref, square_ref, slots_ref, tops_ref, sums_ref, out_ref):
+def half_step(potential, lane_ids_ref, sub_ids_ref, count_ref, square_ref, table_ref, columns_ref, slots_ref, tops_ref, sums_ref, out_ref):
     sub_tiles = potential.shape[0]
     lane_tiles = tops_ref.shape[0] // 8
     scaled = potential * LOG2E
-    if sub_tiles < 128:
-        scaled = jnp.concatenate([scaled, jnp.zeros((128 - sub_tiles, 128), jnp.float32)], axis=0)
-    columns = scaled.T
+    high = scaled.astype(jnp.bfloat16).astype(F32)
+    middle = (scaled - high).astype(jnp.bfloat16).astype(F32)
+    low = scaled - high - middle
+    empty = jnp.zeros((32, 128), F32)
+    for c in range(sub_tiles // 32):
+        at = slice(c * 32, c * 32 + 32)
+        columns_ref[c] = jnp.concatenate([high[at], middle[at], low[at], empty], axis=0).T.astype(jnp.bfloat16)
     count = count_ref[0, 0]
     places = [pl.ds(pl.multiple_of(lane_ids_ref[0, 0, k] * 8, 8), 8) for k in range(SLOTS)]
     tops_ref[...] = jnp.full(tops_ref.shape, NONE, jnp.float32)
     sums_ref[...] = jnp.zeros(sums_ref.shape, jnp.float32)
     for k in range(SLOTS):
         sub = sub_ids_ref[0, 0, k]
-        value = jnp.take_along_axis(columns, jnp.full((128, 128), sub, jnp.int32), axis=1)
+        value = jnp.dot(columns_ref[sub >> 5], table_ref[sub & 31], preferred_element_type=F32)
         score = (value - square_ref[k]).reshape(16, 8, 128)
         peak = jnp.max(score, axis=0)
         total = jnp.sum(jnp.exp2(score - peak[None]), axis=0)
@@ -104,21 +108,28 @@
         out_ref[at : at + 8, :] = jnp.where(top > 0.5 * NONE, top + jnp.log(total), NONE)
 
 
+def make_table(table_ref):
+    row = lax.broadcasted_iota(jnp.int32, (128, 128), 0) & 31
+    for q in range(32):
+        table_ref[q] = (row == q).astype(F32).astype(jnp.bfloat16)
+
+
 def put_total(out_ref, mass):
     rows = out_ref.shape[0]
     total = jnp.sum(jnp.sum(mass.astype(F32), axis=0, keepdims=True), axis=1, keepdims=True)
     out_ref[rows - 8 : rows, :] = jnp.broadcast_to(jnp.log(total), (8, 128))
 
 
-def first_kernel(src_list, tgt_list, count_list, start_in, mass_in, src_in, tgt_in, out, slots, tops, sums, rows, wide, left, right, src_ids, tgt_ids, count, start, mass, src_coords, tgt_coords, square, sems):
+def first_kernel(src_list, tgt_list, count_list, start_in, mass_in, src_in, tgt_in, out, columns, slots, tops, sums, rows, wide, left, right, src_ids, tgt_ids, count, start, mass, src_coords, tgt_coords, square, table, sems):
     pairs = [(src_list, src_ids), (tgt_list, tgt_ids), (count_list, count), (start_in, start), (mass_in, mass), (src_in, src_coords), (tgt_in, tgt_coords)]
     copies = [pltpu.make_async_copy(here, there, sems.at[n]) for n, (here, there) in enumerate(pairs)]
     for copy in copies:
         copy.start()
     for copy in copies:
         copy.wait()
+    make_table(table)
     squares(tgt_coords, src_coords, tgt_ids, src_ids, rows, wide, left, right, square)
-    half_step(start[...], src_ids, tgt_ids, count, square, slots, tops, sums, out)
+    half_step(start[...], src_ids, tgt_ids, count, square, table, columns, slots, tops, sums, out)
     put_total(out, mass[...])
 
 
@@ -126,32 +137,32 @@
     squares(sub_coords, lane_coords, sub_ids, lane_ids, rows, wide, left, right, square)
 
 
-def first_src_kernel(src_ids, tgt_ids, count, m0, m1, m2, m3, src_mass, square, out, tgt_const, slots, tops, sums):
+def first_src_kernel(src_ids, tgt_ids, count, m0, m1, m2, m3, src_mass, square, table, out, tgt_const, columns, slots, tops, sums):
     merged = lse([m0[...], m1[...], m2[...], m3[...]])
     tgt_const[...] = merged[128:136]
     potential = jnp.log(src_mass[...].astype(F32)) - merged[0:128]
-    half_step(potential, tgt_ids, src_ids, count, square, slots, tops, sums, out)
+    half_step(potential, tgt_ids, src_ids, count, square, table, columns, slots, tops, sums, out)
     put_total(out, src_mass[...])
 
 
-def src_kernel(src_ids, tgt_ids, count, m0, m1, m2, m3, src_mass, src_const, square, out, *rest):
-    *pot, slots, tops, sums = rest
+def src_kernel(src_ids, tgt_ids, count, m0, m1, m2, m3, src_mass, src_const, square, table, out, *rest):
+    *pot, columns, slots, tops, sums = rest
     potential = jnp.log(src_mass[...].astype(F32)) - src_const[0:1] - lse([m0[...], m1[...], m2[...], m3[...]])
     if pot:
         pot[0][...] = potential
-    half_step(potential, tgt_ids, src_ids, count, square, slots, tops, sums, out)
-
-
-def first_tgt_kernel(src_ids, tgt_ids, count, m0, m1, m2, m3, tgt_mass, tgt_const, square, out, src_const, slots, tops, sums):
+    half_step(potential, tgt_ids, src_ids, count, square, table, columns, slots, tops, sums, out)
+
+
+def first_tgt_kernel(src_ids, tgt_ids, count, m0, m1, m2, m3, tgt_mass, tgt_const, square, table, out, src_const, columns, slots, tops, sums):
     merged = lse([m0[...], m1[...], m2[...], m3[...]])
     src_const[...] = merged[64:72]
     potential = jnp.log(tgt_mass[...].astype(F32)) - tgt_const[0:1] - (merged[0:64] - merged[64:65])
-    half_step(potential, src_ids, tgt_ids, count, square, slots, tops, sums, out)
-
-
-def tgt_kernel(src_ids, tgt_ids, count, m0, m1, m2, m3, tgt_mass, tgt_const, square, out, slots, tops, sums):
+    half_step(potential, src_ids, tgt_ids, count, square, table, columns, slots, tops, sums, out)
+
+
+def tgt_kernel(src_ids, tgt_ids, count, m0, m1, m2, m3, tgt_mass, tgt_const, square, table, out, columns, slots, tops, sums):
     potential = jnp.log(tgt_mass[...].astype(F32)) - tgt_const[0:1] - lse([m0[...], m1[...], m2[...], m3[...]])
-    half_step(potential, src_ids, tgt_ids, count, square, slots, tops, sums, out)
+    half_step(potential, src_ids, tgt_ids, count, square, table, columns, slots, tops, sums, out)
 
 
 SMEM = pl.BlockSpec(memory_space=pltpu.SMEM)
@@ -163,8 +174,12 @@
 SQUARES = jax.ShapeDtypeStruct((SLOTS, 128, 128), F32)
 
 
+TABLE = jax.ShapeDtypeStruct((32, 128, 128), jnp.bfloat16)
+
+
 def half_scratch(lane_tiles):
-    return [pltpu.VMEM((SLOTS * 8, 128), F32)] + [pltpu.VMEM((lane_tiles * 8, 128), F32)] * 2
+    sub_tiles = 192 - lane_tiles
+    return [pltpu.VMEM((sub_tiles // 32, 128, 128), jnp.bfloat16), pltpu.VMEM((SLOTS * 8, 128), F32)] + [pltpu.VMEM((lane_tiles * 8, 128), F32)] * 2
 
 
 def square_scratch(left_tiles, right_tiles):
@@ -185,7 +200,7 @@
         scratch_shapes=half_scratch(128) + square_scratch(64, 128)
         + [pltpu.SMEM(x.shape, x.dtype) for x in args[:3]]
         + [pltpu.VMEM(x.shape, x.dtype) for x in args[3:]]
-        + [pltpu.VMEM(SQUARES.shape, F32), pltpu.SemaphoreType.DMA((7,))],
+        + [pltpu.VMEM(SQUARES.shape, F32), pltpu.VMEM(TABLE.shape, TABLE.dtype), pltpu.SemaphoreType.DMA((7,))],
     )(*args)
 
 
@@ -194,6 +209,10 @@
         square_kernel, out_shape=SQUARES, in_specs=[SMEM] * 2 + [VMEM] * 2, out_specs=VMEM,
         scratch_shapes=square_scratch(sub_coords.shape[1] // 128, lane_coords.shape[1] // 128), compiler_params=PARAMS,
     )(sub_ids, lane_ids, sub_coords, lane_coords)
+
+
+def table_call():
+    return pl.pallas_call(make_table, out_shape=TABLE, out_specs=VMEM, compiler_params=PARAMS)()
 
 
 def call(body, lane_tiles, outs, *args):
@@ -220,12 +239,10 @@
 
 
 def over_col(message):
-    merged = lse([
-        message,
-        col_permute(message, lambda y, z: (y, z ^ 1)),
-        col_permute(message, lambda y, z: (y ^ 1, z)),
-        col_permute(message, lambda y, z: (y ^ 1, z ^ 1)),
-    ])
+    beside = col_permute(message, lambda y, z: (y, z ^ 1))
+    corner = col_permute(message, lambda y, z: (y ^ 1, z ^ 1))
+    above = col_permute(message, lambda y, z: (y ^ 1, z))
+    merged = lse([message, beside, above, corner])
     merged = lse([merged, col_permute(merged, lambda y, z: (y ^ 3, z))])
     return [merged] + [col_permute(merged, lambda y, z, k=k: (y, z + k if z % 2 else z - k)) for k in (1, 3, -2)]
 
@@ -233,7 +250,8 @@
 def over_row(message):
     other = lax.ppermute(message, "row", [(i, i ^ 1) for i in range(8)])
     merged = lse([message, other])
-    return [merged] + [row_permute(merged, k) for k in (1, 2, 3)]
+    ahead, behind, across = (row_permute(merged, k) for k in (1, 3, 2))
+    return [merged, ahead, across, behind]
 
 
 def on_device(src_coords, tgt_coords, src_mass, tgt_mass, tgt_start, kept_src, kept_tgt, kept_count):
@@ -242,20 +260,21 @@
     lists = (kept_src, kept_tgt, kept_count)
     message = first_call(*lists, tgt_start.reshape(64, 128), tgt_mass, src_coords, tgt_coords)
     tgt_lanes = square_call(kept_src, kept_tgt, src_coords, tgt_coords)
+    table = table_call()
     src_lanes = square_call(kept_tgt, kept_src, tgt_coords, src_coords)
     for iteration in range(ITERS):
         parts = over_col(message)
         if iteration == 0:
-            message, tgt_const = call(first_src_kernel, 64, [72, 8], *lists, *parts, src_mass, tgt_lanes)
+            message, tgt_const = call(first_src_kernel, 64, [72, 8], *lists, *parts, src_mass, tgt_lanes, table)
         elif iteration + 1 < ITERS:
-            (message,) = call(src_kernel, 64, [64], *lists, *parts, src_mass, src_const, tgt_lanes)
+            (message,) = call(src_kernel, 64, [64], *lists, *parts, src_mass, src_const, tgt_lanes, table)
         else:
-            message, src_potential = call(src_kernel, 64, [64, 128], *lists, *parts, src_mass, src_const, tgt_lanes)
+            message, src_potential = call(src_kernel, 64, [64, 128], *lists, *parts, src_mass, src_const, tgt_lanes, table)
         parts = over_row(message)
         if iteration == 0:
-            message, src_const = call(first_tgt_kernel, 128, [128, 8], *lists, *parts, tgt_mass, tgt_const, src_lanes)
+            message, src_const = call(first_tgt_kernel, 128, [128, 8], *lists, *parts, tgt_mass, tgt_const, src_lanes, table)
         elif iteration + 1 < ITERS:
-            (message,) = call(tgt_kernel, 128, [128], *lists, *parts, tgt_mass, tgt_const, src_lanes)
+            (message,) = call(tgt_kernel, 128, [128], *lists, *parts, tgt_mass, tgt_const, src_lanes, table)
     tgt_potential = jnp.log(tgt_mass.astype(F32)) - tgt_const[0:1] - lse(parts)
     return src_potential.reshape(-1), tgt_potential.reshape(-1)
 

time: 124 us -> 122 us (0.984)
  Pallas kernels: 24.1 us -> 21.9 us
    pallas_call x5, Pallas kernels: 13.8 us -> 11.8 us  [call(): pl.pallas_call(body, out_shape=[jax.ShapeDtypeStruct((rows, 128), F32) fo...]
where the time goes in v1:
time: 122 us; the launch traced here: 121 us
  starting transfers between devices  59.6 us (49%)
  waiting for transfers between devices  33.2 us (27%)
  Pallas kernels  21.9 us (18%)
  local copies, waits for them, and re-layouts  3.17 us (3%)
  other arithmetic  1.96 us (2%)
  between operations  1.49 us (1%)
    ppermute x21, starting transfers between devices, col_permute(): return lax.ppermute(value, 'col', pairs)  34.5 us
    ppermute x21, waiting for transfers between devices, col_permute(): return lax.ppermute(value, 'col', pairs)  25.2 us
    ppermute x3, starting transfers between devices, over_row(): other = lax.ppermute(message, 'row', [(i, i ^ 1) for i in range(8)])  13.3 us
    pallas_call x5, Pallas kernels, call(): pl.pallas_call(body, out_shape=[jax.ShapeDtypeStruct((rows, 128), F32) fo...  11.8 us
    ppermute x9, starting transfers between devices, row_permute(): lax.ppermute(value, 'row', [(i, (i + 2 * shift) % 8) for i in range(8)])  11.8 us
    ppermute x9, waiting for transfers between devices, row_permute(): lax.ppermute(value, 'row', [(i, (i + 2 * shift) % 8) for i in range(8)])  5.37 us
    pallas_call x1, Pallas kernels, first_call(): pl.pallas_call(first_kernel, out_shape=jax.ShapeDtypeStruct((136, 128), F...  5.27 us
    pallas_call x2, Pallas kernels, square_call(): pl.pallas_call(square_kernel, out_shape=SQUARES, in_specs=[SMEM] * 2 + [V...  4.69 us
  transfers between devices with their start and end apart: 33, of which 28 were waited for; matrix products, arithmetic and copies ran while one was open for 0% of the time, Pallas kernels for 4%

profile of v1, /device:TPU:1, one launch (start us, length us, event | category | flops | bytes accessed | tf_op | source)
XLA Modules:
  0.0 121.3 jit_solution(10210142914990957328)
XLA Ops:
  1.3 5.3 %shard_map.95 = f32[136,128]{1,0:T(8,128)} custom-call(s32[1,1,64]{2,1,0:T(1,128)} %src_ids.9, s32[1,1,64]{2,1,0:T(1,128)} %tgt_ids.9, s32[1,1]{1,0:T(1,128)S(6)} %copy.10.count_list.count, f32[64,128]{1,0:T(8,128)} %bitcast.15, s32[64,128]{1,0:T(8,128)} %bitcast.12, s32[3,16384]{1,0:T(4,128)} %lane_coords.3, s32[3,8192]{1,0:T(4,128)} %sub_coords.3), custom_call_target="tpu_custom_call" | custom-call | tf_op jit(solution)/shard_map/pallas_call | solution.py:195
  6.6 2.5 %collective-permute-start = (f32[136,128]{1,0:T(8,128)}, f32[136,128]{1,0:T(8,128)S(1)}, u32[]{:S(2)}, u32[]{:S(2)}) collective-permute-start(f32[136,128]{1,0:T(8,128)} %shard_map.95), channel_id=1, source_target_pairs={{1,0},{0,1},{3,2},{2,3},{5,4},{4,5},{7,6},{6,7},{9,8},{8,9},{11,10... | collective-permute-start | bytes 208904 | tf_op jit(solution)/shard_map/ppermute | solution.py:234
  12.5 2.2 %collective-permute-done.2 = f32[136,128]{1,0:T(8,128)S(1)} collective-permute-done((f32[136,128]{1,0:T(8,128)}, f32[136,128]{1,0:T(8,128)S(1)}, u32[]{:S(2)}, u32[]{:S(2)}) %collective-permute-start.2) | collective-permute-done | bytes 69664 | tf_op jit(solution)/shard_map/ppermute | solution.py:234
  15.7 2.1 %collective-permute-start.3 = (f32[136,128]{1,0:T(8,128)S(1)}, f32[136,128]{1,0:T(8,128)S(1)}, u32[]{:S(2)}, u32[]{:S(2)}) collective-permute-start(f32[136,128]{1,0:T(8,128)S(1)} %log_add_fusion.1), channel_id=1, source_target_pairs={{24,0},{25,1},{26,2},{27,3},{28,4},{29,5},{30,6},{31,7},{16,8},{17... | collective-permute-start | bytes 208904 | tf_op jit(solution)/shard_map/ppermute | solution.py:234
  17.7 2.4 %collective-permute-done.3 = f32[136,128]{1,0:T(8,128)S(1)} collective-permute-done((f32[136,128]{1,0:T(8,128)S(1)}, f32[136,128]{1,0:T(8,128)S(1)}, u32[]{:S(2)}, u32[]{:S(2)}) %collective-permute-start.3) | collective-permute-done | bytes 69664 | tf_op jit(solution)/shard_map/ppermute | solution.py:234
  20.2 4.8 %collective-permute-start.4 = (f32[136,128]{1,0:T(8,128)S(1)}, f32[136,128]{1,0:T(8,128)S(1)}, u32[]{:S(2)}, u32[]{:S(2)}) collective-permute-start(f32[136,128]{1,0:T(8,128)S(1)} %log_add_fusion.m0), channel_id=1, source_target_pairs={{7,0},{2,1},{1,2},{4,3},{3,4},{6,5},{5,6},{0,7},{15,8},{10,9},{9,1... | collective-permute-start | bytes 208904 | tf_op jit(solution)/shard_map/ppermute | solution.py:234
  26.6 2.4 %collective-permute-start.6 = (f32[136,128]{1,0:T(8,128)S(1)}, f32[136,128]{1,0:T(8,128)S(1)}, u32[]{:S(2)}, u32[]{:S(2)}) collective-permute-start(f32[136,128]{1,0:T(8,128)S(1)} %log_add_fusion.m0), channel_id=1, source_target_pairs={{2,0},{7,1},{4,2},{1,3},{6,4},{3,5},{0,6},{5,7},{10,8},{15,9},{12,... | collective-permute-start | bytes 208904 | tf_op jit(solution)/shard_map/ppermute | solution.py:234
  32.3 2.4 %shard_map.96.square = f32[64,128,128]{2,1,0:T(8,128)S(1)} custom-call(s32[1,1,64]{2,1,0:T(1,128)S(1)} %copy-done.4, s32[1,1,64]{2,1,0:T(1,128)S(1)} %copy-done.5, s32[3,16384]{1,0:T(4,128)S(1)} %copy-done, s32[3,8192]{1,0:T(4,128)S(1)} %copy-done.1), custom_call_target="tpu_custom_call" | custom-call | tf_op jit(solution)/shard_map/pallas_call | solution.py:208
  34.7 2.3 %shard_map.98 = (f32[72,128]{1,0:T(8,128)S(1)}, f32[8,128]{1,0:T(8,128)S(1)}) custom-call(s32[1,1,64]{2,1,0:T(1,128)S(1)} %copy-done.4, s32[1,1,64]{2,1,0:T(1,128)S(1)} %copy-done.5, s32[1,1]{1,0:T(1,128)S(6)} %copy.10.count_list.count, f32[136,128]{1,0:T(8,128)S(1)} %log_add_fusion.m0, f32[136,128]{1,0:T(8,128)S(1)} %collective-permute-done.4.m1, ...), custom_call_target="tpu_custom_call" | custom-call | tf_op jit(solution)/shard_map/pallas_call | solution.py:219
  37.0 4.4 %collective-permute-start.7 = (f32[72,128]{1,0:T(8,128)S(1)}, f32[72,128]{1,0:T(8,128)S(1)}, u32[]{:S(2)}, u32[]{:S(2)}) collective-permute-start(f32[72,128]{1,0:T(8,128)S(1)} %get-tuple-element.8), channel_id=1, source_target_pairs={{0,32},{32,0},{64,96},{96,64},{128,160},{160,128},{192,224},{224,1... | collective-permute-start | bytes 110600 | tf_op jit(solution)/shard_map/ppermute | solution.py:251
  42.3 2.6 %collective-permute-start.10 = (f32[72,128]{1,0:T(8,128)S(1)}, f32[72,128]{1,0:T(8,128)S(1)}, u32[]{:S(2)}, u32[]{:S(2)}) collective-permute-start(f32[72,128]{1,0:T(8,128)S(1)} %log_add_fusion.6.m0), channel_id=1, source_target_pairs={{0,192},{32,224},{64,0},{96,32},{128,64},{160,96},{192,128},{224,1... | collective-permute-start | bytes 110600 | tf_op jit(solution)/shard_map/ppermute | solution.py:238
  44.9 1.7 %collective-permute-start.9 = (f32[72,128]{1,0:T(8,128)S(1)}, f32[72,128]{1,0:T(8,128)S(1)}, u32[]{:S(2)}, u32[]{:S(2)}) collective-permute-start(f32[72,128]{1,0:T(8,128)S(1)} %log_add_fusion.6.m0), channel_id=1, source_target_pairs={{0,128},{32,160},{64,192},{96,224},{128,0},{160,32},{192,64},{224,... | collective-permute-start | bytes 110600 | tf_op jit(solution)/shard_map/ppermute | solution.py:238
  46.6 2.3 %shard_map.99.square = f32[64,128,128]{2,1,0:T(8,128)S(1)} custom-call(s32[1,1,64]{2,1,0:T(1,128)S(1)} %copy-done.5, s32[1,1,64]{2,1,0:T(1,128)S(1)} %copy-done.4, s32[3,8192]{1,0:T(4,128)S(1)} %copy-done.1, s32[3,16384]{1,0:T(4,128)S(1)} %copy-done), custom_call_target="tpu_custom_call" | custom-call | tf_op jit(solution)/shard_map/pallas_call | solution.py:208
  49.4 2.3 %shard_map.100 = (f32[128,128]{1,0:T(8,128)S(1)}, f32[8,128]{1,0:T(8,128)S(1)}) custom-call(s32[1,1,64]{2,1,0:T(1,128)S(1)} %copy-done.4, s32[1,1,64]{2,1,0:T(1,128)S(1)} %copy-done.5, s32[1,1]{1,0:T(1,128)S(6)} %copy.10.count_list.count, f32[72,128]{1,0:T(8,128)S(1)} %log_add_fusion.6.m0, f32[72,128]{1,0:T(8,128)S(1)} %collective-permute-done.8.m1, ...), custom_call_target="tpu_custom_call" | custom-call | tf_op jit(solution)/shard_map/pallas_call | solution.py:219
  51.9 2.5 %collective-permute-start.13 = (f32[128,128]{1,0:T(8,128)S(1)}, f32[128,128]{1,0:T(8,128)S(1)}, u32[]{:S(2)}, u32[]{:S(2)}) collective-permute-start(f32[128,128]{1,0:T(8,128)S(1)} %get-tuple-element.10), channel_id=1, source_target_pairs={{9,0},{8,1},{11,2},{10,3},{13,4},{12,5},{15,6},{14,7},{1,8},{0,9},... | collective-permute-start | bytes 196616 | tf_op jit(solution)/shard_map/ppermute | solution.py:234
  55.0 1.9 %collective-permute-done.13 = f32[128,128]{1,0:T(8,128)S(1)} collective-permute-done((f32[128,128]{1,0:T(8,128)S(1)}, f32[128,128]{1,0:T(8,128)S(1)}, u32[]{:S(2)}, u32[]{:S(2)}) %collective-permute-start.13) | collective-permute-done | bytes 65568 | tf_op jit(solution)/shard_map/ppermute | solution.py:234
  58.5 2.8 %collective-permute-done.14 = f32[128,128]{1,0:T(8,128)S(1)} collective-permute-done((f32[128,128]{1,0:T(8,128)S(1)}, f32[128,128]{1,0:T(8,128)S(1)}, u32[]{:S(2)}, u32[]{:S(2)}) %collective-permute-start.14) | collective-permute-done | bytes 65568 | tf_op jit(solution)/shard_map/ppermute | solution.py:234
  62.9 2.7 %collective-permute-start.17 = (f32[128,128]{1,0:T(8,128)S(1)}, f32[128,128]{1,0:T(8,128)S(1)}, u32[]{:S(2)}, u32[]{:S(2)}) collective-permute-start(f32[128,128]{1,0:T(8,128)S(1)} %log_add_fusion.4.m0), channel_id=1, source_target_pairs={{2,0},{7,1},{4,2},{1,3},{6,4},{3,5},{0,6},{5,7},{10,8},{15,9},{12,... | collective-permute-start | bytes 196616 | tf_op jit(solution)/shard_map/ppermute | solution.py:234
  65.8 2.0 %collective-permute-done.16.m2 = f32[128,128]{1,0:T(8,128)S(1)} collective-permute-done((f32[128,128]{1,0:T(8,128)S(1)}, f32[128,128]{1,0:T(8,128)S(1)}, u32[]{:S(2)}, u32[]{:S(2)}) %collective-permute-start.16) | collective-permute-done | bytes 65568 | tf_op jit(solution)/shard_map/ppermute | solution.py:234
  67.8 2.3 %collective-permute-done.17.m3 = f32[128,128]{1,0:T(8,128)S(1)} collective-permute-done((f32[128,128]{1,0:T(8,128)S(1)}, f32[128,128]{1,0:T(8,128)S(1)}, u32[]{:S(2)}, u32[]{:S(2)}) %collective-permute-start.17) | collective-permute-done | bytes 65568 | tf_op jit(solution)/shard_map/ppermute | solution.py:234
  70.1 2.2 %shard_map.101 = f32[64,128]{1,0:T(8,128)S(1)} custom-call(s32[1,1,64]{2,1,0:T(1,128)S(1)} %copy-done.4, s32[1,1,64]{2,1,0:T(1,128)S(1)} %copy-done.5, s32[1,1]{1,0:T(1,128)S(6)} %copy.10.count_list.count, f32[128,128]{1,0:T(8,128)S(1)} %log_add_fusion.4.m0, f32[128,128]{1,0:T(8,128)S(1)} %collective-permute-done.15.m1, ...), custom_call_target="tpu_custom_call" | custom-call | tf_op jit(solution)/shard_map/pallas_call | solution.py:219
  72.4 3.4 %collective-permute-start.18 = (f32[64,128]{1,0:T(8,128)S(1)}, f32[64,128]{1,0:T(8,128)S(1)}, u32[]{:S(2)}, u32[]{:S(2)}) collective-permute-start(f32[64,128]{1,0:T(8,128)S(1)} %shard_map.101), channel_id=1, source_target_pairs={{0,32},{32,0},{64,96},{96,64},{128,160},{160,128},{192,224},{224,1... | collective-permute-start | bytes 98312 | tf_op jit(solution)/shard_map/ppermute | solution.py:251
  77.4 3.4 %collective-permute-start.20 = (f32[64,128]{1,0:T(8,128)S(1)}, f32[64,128]{1,0:T(8,128)S(1)}, u32[]{:S(2)}, u32[]{:S(2)}) collective-permute-start(f32[64,128]{1,0:T(8,128)S(1)} %log_add_fusion.8.m0), channel_id=1, source_target_pairs={{0,128},{32,160},{64,192},{96,224},{128,0},{160,32},{192,64},{224,... | collective-permute-start | bytes 98312 | tf_op jit(solution)/shard_map/ppermute | solution.py:238
  83.6 2.3 %shard_map.102 = f32[128,128]{1,0:T(8,128)S(1)} custom-call(s32[1,1,64]{2,1,0:T(1,128)S(1)} %copy-done.4, s32[1,1,64]{2,1,0:T(1,128)S(1)} %copy-done.5, s32[1,1]{1,0:T(1,128)S(6)} %copy.10.count_list.count, f32[64,128]{1,0:T(8,128)S(1)} %log_add_fusion.8.m0, f32[64,128]{1,0:T(8,128)S(1)} %collective-permute-done.19.m1, ...), custom_call_target="tpu_custom_call" | custom-call | tf_op jit(solution)/shard_map/pallas_call | solution.py:219
  85.8 2.8 %collective-permute-start.22 = (f32[128,128]{1,0:T(8,128)S(1)}, f32[128,128]{1,0:T(8,128)S(1)}, u32[]{:S(2)}, u32[]{:S(2)}) collective-permute-start(f32[128,128]{1,0:T(8,128)S(1)} %shard_map.102), channel_id=1, source_target_pairs={{1,0},{0,1},{3,2},{2,3},{5,4},{4,5},{7,6},{6,7},{9,8},{8,9},{11,10... | collective-permute-start | bytes 196616 | tf_op jit(solution)/shard_map/ppermute | solution.py:234
  93.1 2.0 %collective-permute-start.25 = (f32[128,128]{1,0:T(8,128)S(1)}, f32[128,128]{1,0:T(8,128)S(1)}, u32[]{:S(2)}, u32[]{:S(2)}) collective-permute-start(f32[128,128]{1,0:T(8,128)S(1)} %log_add_fusion.3), channel_id=1, source_target_pairs={{24,0},{25,1},{26,2},{27,3},{28,4},{29,5},{30,6},{31,7},{16,8},{17... | collective-permute-start | bytes 196616 | tf_op jit(solution)/shard_map/ppermute | solution.py:234
  95.1 2.4 %collective-permute-done.25 = f32[128,128]{1,0:T(8,128)S(1)} collective-permute-done((f32[128,128]{1,0:T(8,128)S(1)}, f32[128,128]{1,0:T(8,128)S(1)}, u32[]{:S(2)}, u32[]{:S(2)}) %collective-permute-start.25) | collective-permute-done | bytes 65568 | tf_op jit(solution)/shard_map/ppermute | solution.py:234
  99.4 3.4 %collective-permute-start.28 = (f32[128,128]{1,0:T(8,128)S(1)}, f32[128,128]{1,0:T(8,128)S(1)}, u32[]{:S(2)}, u32[]{:S(2)}) collective-permute-start(f32[128,128]{1,0:T(8,128)S(1)} %log_add_fusion.2.m0), channel_id=1, source_target_pairs={{2,0},{7,1},{4,2},{1,3},{6,4},{3,5},{0,6},{5,7},{10,8},{15,9},{12,... | collective-permute-start | bytes 196616 | tf_op jit(solution)/shard_map/ppermute | solution.py:234
  102.8 2.8 %collective-permute-done.27.m2 = f32[128,128]{1,0:T(8,128)S(1)} collective-permute-done((f32[128,128]{1,0:T(8,128)S(1)}, f32[128,128]{1,0:T(8,128)S(1)}, u32[]{:S(2)}, u32[]{:S(2)}) %collective-permute-start.27) | collective-permute-done | bytes 65568 | tf_op jit(solution)/shard_map/ppermute | solution.py:234
  106.0 2.7 %shard_map.103 = (f32[64,128]{1,0:T(8,128)S(1)}, f32[128,128]{1,0:T(8,128)}) custom-call(s32[1,1,64]{2,1,0:T(1,128)S(1)} %copy-done.4, s32[1,1,64]{2,1,0:T(1,128)S(1)} %copy-done.5, s32[1,1]{1,0:T(1,128)S(6)} %copy.10.count_list.count, f32[128,128]{1,0:T(8,128)S(1)} %log_add_fusion.2.m0, f32[128,128]{1,0:T(8,128)S(1)} %collective-permute-done.26.m1, ...), custom_call_target="tpu_custom_call" | custom-call | tf_op jit(solution)/shard_map/pallas_call | solution.py:219
  108.8 5.4 %collective-permute-start.29 = (f32[64,128]{1,0:T(8,128)S(1)}, f32[64,128]{1,0:T(8,128)S(1)}, u32[]{:S(2)}, u32[]{:S(2)}) collective-permute-start(f32[64,128]{1,0:T(8,128)S(1)} %get-tuple-element.13), channel_id=1, source_target_pairs={{0,32},{32,0},{64,96},{96,64},{128,160},{160,128},{192,224},{224,1... | collective-permute-start | bytes 98312 | tf_op jit(solution)/shard_map/ppermute | solution.py:251
  115.2 2.3 %collective-permute-start.31 = (f32[64,128]{1,0:T(8,128)S(1)}, f32[64,128]{1,0:T(8,128)S(1)}, u32[]{:S(2)}, u32[]{:S(2)}) collective-permute-start(f32[64,128]{1,0:T(8,128)S(1)} %log_add_fusion.7), channel_id=1, source_target_pairs={{0,128},{32,160},{64,192},{96,224},{128,0},{160,32},{192,64},{224,... | collective-permute-start | bytes 98312 | tf_op jit(solution)/shard_map/ppermute | solution.py:238
  (66 shorter events, 30.7 us)
Async XLA Ops:
  6.6 4.5 %collective-permute-start = (f32[136,128]{1,0:T(8,128)}, f32[136,128]{1,0:T(8,128)S(1)}, u32[]{:S(2)}, u32[]{:S(2)}) collective-permute-start(f32[136,128]{1,0:T(8,128)} %shard_map.95), channel_id=1, source_target_pairs={{1,0},{0,1},{3,2},{2,3},{5,4},{4,5},{7,6},{6,7},{9,8},{8,9},{11,10... | collective-permute-start | bytes 208904 | tf_op jit(solution)/shard_map/ppermute | solution.py:234
  9.1 3.4 %collective-permute-start.1 = (f32[136,128]{1,0:T(8,128)}, f32[136,128]{1,0:T(8,128)S(1)}, u32[]{:S(2)}, u32[]{:S(2)}) collective-permute-start(f32[136,128]{1,0:T(8,128)} %shard_map.95), channel_id=1, source_target_pairs={{8,0},{9,1},{10,2},{11,3},{12,4},{13,5},{14,6},{15,7},{0,8},{1,9},... | collective-permute-start | bytes 208904 | tf_op jit(solution)/shard_map/ppermute | solution.py:234
  10.4 4.3 %collective-permute-start.2 = (f32[136,128]{1,0:T(8,128)}, f32[136,128]{1,0:T(8,128)S(1)}, u32[]{:S(2)}, u32[]{:S(2)}) collective-permute-start(f32[136,128]{1,0:T(8,128)} %shard_map.95), channel_id=1, source_target_pairs={{9,0},{8,1},{11,2},{10,3},{13,4},{12,5},{15,6},{14,7},{1,8},{0,9},... | collective-permute-start | bytes 208904 | tf_op jit(solution)/shard_map/ppermute | solution.py:234
  15.7 4.5 %collective-permute-start.3 = (f32[136,128]{1,0:T(8,128)S(1)}, f32[136,128]{1,0:T(8,128)S(1)}, u32[]{:S(2)}, u32[]{:S(2)}) collective-permute-start(f32[136,128]{1,0:T(8,128)S(1)} %log_add_fusion.1), channel_id=1, source_target_pairs={{24,0},{25,1},{26,2},{27,3},{28,4},{29,5},{30,6},{31,7},{16,8},{17... | collective-permute-start | bytes 208904 | tf_op jit(solution)/shard_map/ppermute | solution.py:234
  20.2 14.5 %collective-permute-start.4 = (f32[136,128]{1,0:T(8,128)S(1)}, f32[136,128]{1,0:T(8,128)S(1)}, u32[]{:S(2)}, u32[]{:S(2)}) collective-permute-start(f32[136,128]{1,0:T(8,128)S(1)} %log_add_fusion.m0), channel_id=1, source_target_pairs={{7,0},{2,1},{1,2},{4,3},{3,4},{6,5},{5,6},{0,7},{15,8},{10,9},{9,1... | collective-permute-start | bytes 208904 | tf_op jit(solution)/shard_map/ppermute | solution.py:234
  24.9 9.8 %collective-permute-start.5 = (f32[136,128]{1,0:T(8,128)S(1)}, f32[136,128]{1,0:T(8,128)S(1)}, u32[]{:S(2)}, u32[]{:S(2)}) collective-permute-start(f32[136,128]{1,0:T(8,128)S(1)} %log_add_fusion.m0), channel_id=1, source_target_pairs={{5,0},{4,1},{7,2},{6,3},{1,4},{0,5},{3,6},{2,7},{13,8},{12,9},{15,... | collective-permute-start | bytes 208904 | tf_op jit(solution)/shard_map/ppermute | solution.py:234
  26.6 8.2 %collective-permute-start.6 = (f32[136,128]{1,0:T(8,128)S(1)}, f32[136,128]{1,0:T(8,128)S(1)}, u32[]{:S(2)}, u32[]{:S(2)}) collective-permute-start(f32[136,128]{1,0:T(8,128)S(1)} %log_add_fusion.m0), channel_id=1, source_target_pairs={{2,0},{7,1},{4,2},{1,3},{6,4},{3,5},{0,6},{5,7},{10,8},{15,9},{12,... | collective-permute-start | bytes 208904 | tf_op jit(solution)/shard_map/ppermute | solution.py:234
  37.0 5.3 %collective-permute-start.7 = (f32[72,128]{1,0:T(8,128)S(1)}, f32[72,128]{1,0:T(8,128)S(1)}, u32[]{:S(2)}, u32[]{:S(2)}) collective-permute-start(f32[72,128]{1,0:T(8,128)S(1)} %get-tuple-element.8), channel_id=1, source_target_pairs={{0,32},{32,0},{64,96},{96,64},{128,160},{160,128},{192,224},{224,1... | collective-permute-start | bytes 110600 | tf_op jit(solution)/shard_map/ppermute | solution.py:251
  42.3 6.6 %collective-permute-start.10 = (f32[72,128]{1,0:T(8,128)S(1)}, f32[72,128]{1,0:T(8,128)S(1)}, u32[]{:S(2)}, u32[]{:S(2)}) collective-permute-start(f32[72,128]{1,0:T(8,128)S(1)} %log_add_fusion.6.m0), channel_id=1, source_target_pairs={{0,192},{32,224},{64,0},{96,32},{128,64},{160,96},{192,128},{224,1... | collective-permute-start | bytes 110600 | tf_op jit(solution)/shard_map/ppermute | solution.py:238
  44.9 4.1 %collective-permute-start.8 = (f32[72,128]{1,0:T(8,128)S(1)}, f32[72,128]{1,0:T(8,128)S(1)}, u32[]{:S(2)}, u32[]{:S(2)}) collective-permute-start(f32[72,128]{1,0:T(8,128)S(1)} %log_add_fusion.6.m0), channel_id=1, source_target_pairs={{0,64},{32,96},{64,128},{96,160},{128,192},{160,224},{192,0},{224,... | collective-permute-start | bytes 110600 | tf_op jit(solution)/shard_map/ppermute | solution.py:238
  44.9 4.6 %collective-permute-start.9 = (f32[72,128]{1,0:T(8,128)S(1)}, f32[72,128]{1,0:T(8,128)S(1)}, u32[]{:S(2)}, u32[]{:S(2)}) collective-permute-start(f32[72,128]{1,0:T(8,128)S(1)} %log_add_fusion.6.m0), channel_id=1, source_target_pairs={{0,128},{32,160},{64,192},{96,224},{128,0},{160,32},{192,64},{224,... | collective-permute-start | bytes 110600 | tf_op jit(solution)/shard_map/ppermute | solution.py:238
  51.7 3.2 %collective-permute-start.11 = (f32[128,128]{1,0:T(8,128)S(1)}, f32[128,128]{1,0:T(8,128)S(1)}, u32[]{:S(2)}, u32[]{:S(2)}) collective-permute-start(f32[128,128]{1,0:T(8,128)S(1)} %get-tuple-element.10), channel_id=1, source_target_pairs={{1,0},{0,1},{3,2},{2,3},{5,4},{4,5},{7,6},{6,7},{9,8},{8,9},{11,10... | collective-permute-start | bytes 196616 | tf_op jit(solution)/shard_map/ppermute | solution.py:234
  51.8 3.2 %collective-permute-start.12 = (f32[128,128]{1,0:T(8,128)S(1)}, f32[128,128]{1,0:T(8,128)S(1)}, u32[]{:S(2)}, u32[]{:S(2)}) collective-permute-start(f32[128,128]{1,0:T(8,128)S(1)} %get-tuple-element.10), channel_id=1, source_target_pairs={{8,0},{9,1},{10,2},{11,3},{12,4},{13,5},{14,6},{15,7},{0,8},{1,9},... | collective-permute-start | bytes 196616 | tf_op jit(solution)/shard_map/ppermute | solution.py:234
  51.9 5.0 %collective-permute-start.13 = (f32[128,128]{1,0:T(8,128)S(1)}, f32[128,128]{1,0:T(8,128)S(1)}, u32[]{:S(2)}, u32[]{:S(2)}) collective-permute-start(f32[128,128]{1,0:T(8,128)S(1)} %get-tuple-element.10), channel_id=1, source_target_pairs={{9,0},{8,1},{11,2},{10,3},{13,4},{12,5},{15,6},{14,7},{1,8},{0,9},... | collective-permute-start | bytes 196616 | tf_op jit(solution)/shard_map/ppermute | solution.py:234
  57.0 4.4 %collective-permute-start.14 = (f32[128,128]{1,0:T(8,128)S(1)}, f32[128,128]{1,0:T(8,128)S(1)}, u32[]{:S(2)}, u32[]{:S(2)}) collective-permute-start(f32[128,128]{1,0:T(8,128)S(1)} %log_add_fusion.5), channel_id=1, source_target_pairs={{24,0},{25,1},{26,2},{27,3},{28,4},{29,5},{30,6},{31,7},{16,8},{17... | collective-permute-start | bytes 196616 | tf_op jit(solution)/shard_map/ppermute | solution.py:234
  61.4 4.4 %collective-permute-start.15 = (f32[128,128]{1,0:T(8,128)S(1)}, f32[128,128]{1,0:T(8,128)S(1)}, u32[]{:S(2)}, u32[]{:S(2)}) collective-permute-start(f32[128,128]{1,0:T(8,128)S(1)} %log_add_fusion.4.m0), channel_id=1, source_target_pairs={{7,0},{2,1},{1,2},{4,3},{3,4},{6,5},{5,6},{0,7},{15,8},{10,9},{9,1... | collective-permute-start | bytes 196616 | tf_op jit(solution)/shard_map/ppermute | solution.py:234
  61.5 6.3 %collective-permute-start.16 = (f32[128,128]{1,0:T(8,128)S(1)}, f32[128,128]{1,0:T(8,128)S(1)}, u32[]{:S(2)}, u32[]{:S(2)}) collective-permute-start(f32[128,128]{1,0:T(8,128)S(1)} %log_add_fusion.4.m0), channel_id=1, source_target_pairs={{5,0},{4,1},{7,2},{6,3},{1,4},{0,5},{3,6},{2,7},{13,8},{12,9},{15,... | collective-permute-start | bytes 196616 | tf_op jit(solution)/shard_map/ppermute | solution.py:234
  62.9 7.2 %collective-permute-start.17 = (f32[128,128]{1,0:T(8,128)S(1)}, f32[128,128]{1,0:T(8,128)S(1)}, u32[]{:S(2)}, u32[]{:S(2)}) collective-permute-start(f32[128,128]{1,0:T(8,128)S(1)} %log_add_fusion.4.m0), channel_id=1, source_target_pairs={{2,0},{7,1},{4,2},{1,3},{6,4},{3,5},{0,6},{5,7},{10,8},{15,9},{12,... | collective-permute-start | bytes 196616 | tf_op jit(solution)/shard_map/ppermute | solution.py:234
  72.4 4.3 %collective-permute-start.18 = (f32[64,128]{1,0:T(8,128)S(1)}, f32[64,128]{1,0:T(8,128)S(1)}, u32[]{:S(2)}, u32[]{:S(2)}) collective-permute-start(f32[64,128]{1,0:T(8,128)S(1)} %shard_map.101), channel_id=1, source_target_pairs={{0,32},{32,0},{64,96},{96,64},{128,160},{160,128},{192,224},{224,1... | collective-permute-start | bytes 98312 | tf_op jit(solution)/shard_map/ppermute | solution.py:251
  76.7 4.2 %collective-permute-start.19 = (f32[64,128]{1,0:T(8,128)S(1)}, f32[64,128]{1,0:T(8,128)S(1)}, u32[]{:S(2)}, u32[]{:S(2)}) collective-permute-start(f32[64,128]{1,0:T(8,128)S(1)} %log_add_fusion.8.m0), channel_id=1, source_target_pairs={{0,64},{32,96},{64,128},{96,160},{128,192},{160,224},{192,0},{224,... | collective-permute-start | bytes 98312 | tf_op jit(solution)/shard_map/ppermute | solution.py:238
  77.4 5.1 %collective-permute-start.20 = (f32[64,128]{1,0:T(8,128)S(1)}, f32[64,128]{1,0:T(8,128)S(1)}, u32[]{:S(2)}, u32[]{:S(2)}) collective-permute-start(f32[64,128]{1,0:T(8,128)S(1)} %log_add_fusion.8.m0), channel_id=1, source_target_pairs={{0,128},{32,160},{64,192},{96,224},{128,0},{160,32},{192,64},{224,... | collective-permute-start | bytes 98312 | tf_op jit(solution)/shard_map/ppermute | solution.py:238
  85.8 4.4 %collective-permute-start.22 = (f32[128,128]{1,0:T(8,128)S(1)}, f32[128,128]{1,0:T(8,128)S(1)}, u32[]{:S(2)}, u32[]{:S(2)}) collective-permute-start(f32[128,128]{1,0:T(8,128)S(1)} %shard_map.102), channel_id=1, source_target_pairs={{1,0},{0,1},{3,2},{2,3},{5,4},{4,5},{7,6},{6,7},{9,8},{8,9},{11,10... | collective-permute-start | bytes 196616 | tf_op jit(solution)/shard_map/ppermute | solution.py:234
  88.6 3.1 %collective-permute-start.23 = (f32[128,128]{1,0:T(8,128)S(1)}, f32[128,128]{1,0:T(8,128)S(1)}, u32[]{:S(2)}, u32[]{:S(2)}) collective-permute-start(f32[128,128]{1,0:T(8,128)S(1)} %shard_map.102), channel_id=1, source_target_pairs={{8,0},{9,1},{10,2},{11,3},{12,4},{13,5},{14,6},{15,7},{0,8},{1,9},... | collective-permute-start | bytes 196616 | tf_op jit(solution)/shard_map/ppermute | solution.py:234
  88.7 4.3 %collective-permute-start.24 = (f32[128,128]{1,0:T(8,128)S(1)}, f32[128,128]{1,0:T(8,128)S(1)}, u32[]{:S(2)}, u32[]{:S(2)}) collective-permute-start(f32[128,128]{1,0:T(8,128)S(1)} %shard_map.102), channel_id=1, source_target_pairs={{9,0},{8,1},{11,2},{10,3},{13,4},{12,5},{15,6},{14,7},{1,8},{0,9},... | collective-permute-start | bytes 196616 | tf_op jit(solution)/shard_map/ppermute | solution.py:234
  93.1 4.4 %collective-permute-start.25 = (f32[128,128]{1,0:T(8,128)S(1)}, f32[128,128]{1,0:T(8,128)S(1)}, u32[]{:S(2)}, u32[]{:S(2)}) collective-permute-start(f32[128,128]{1,0:T(8,128)S(1)} %log_add_fusion.3), channel_id=1, source_target_pairs={{24,0},{25,1},{26,2},{27,3},{28,4},{29,5},{30,6},{31,7},{16,8},{17... | collective-permute-start | bytes 196616 | tf_op jit(solution)/shard_map/ppermute | solution.py:234
  97.5 5.2 %collective-permute-start.26 = (f32[128,128]{1,0:T(8,128)S(1)}, f32[128,128]{1,0:T(8,128)S(1)}, u32[]{:S(2)}, u32[]{:S(2)}) collective-permute-start(f32[128,128]{1,0:T(8,128)S(1)} %log_add_fusion.2.m0), channel_id=1, source_target_pairs={{7,0},{2,1},{1,2},{4,3},{3,4},{6,5},{5,6},{0,7},{15,8},{10,9},{9,1... | collective-permute-start | bytes 196616 | tf_op jit(solution)/shard_map/ppermute | solution.py:234
  98.7 6.8 %collective-permute-start.27 = (f32[128,128]{1,0:T(8,128)S(1)}, f32[128,128]{1,0:T(8,128)S(1)}, u32[]{:S(2)}, u32[]{:S(2)}) collective-permute-start(f32[128,128]{1,0:T(8,128)S(1)} %log_add_fusion.2.m0), channel_id=1, source_target_pairs={{5,0},{4,1},{7,2},{6,3},{1,4},{0,5},{3,6},{2,7},{13,8},{12,9},{15,... | collective-permute-start | bytes 196616 | tf_op jit(solution)/shard_map/ppermute | solution.py:234
  99.4 6.6 %collective-permute-start.28 = (f32[128,128]{1,0:T(8,128)S(1)}, f32[128,128]{1,0:T(8,128)S(1)}, u32[]{:S(2)}, u32[]{:S(2)}) collective-permute-start(f32[128,128]{1,0:T(8,128)S(1)} %log_add_fusion.2.m0), channel_id=1, source_target_pairs={{2,0},{7,1},{4,2},{1,3},{6,4},{3,5},{0,6},{5,7},{10,8},{15,9},{12,... | collective-permute-start | bytes 196616 | tf_op jit(solution)/shard_map/ppermute | solution.py:234
  108.8 6.3 %collective-permute-start.29 = (f32[64,128]{1,0:T(8,128)S(1)}, f32[64,128]{1,0:T(8,128)S(1)}, u32[]{:S(2)}, u32[]{:S(2)}) collective-permute-start(f32[64,128]{1,0:T(8,128)S(1)} %get-tuple-element.13), channel_id=1, source_target_pairs={{0,32},{32,0},{64,96},{96,64},{128,160},{160,128},{192,224},{224,1... | collective-permute-start | bytes 98312 | tf_op jit(solution)/shard_map/ppermute | solution.py:251
  115.1 4.1 %collective-permute-start.30 = (f32[64,128]{1,0:T(8,128)S(1)}, f32[64,128]{1,0:T(8,128)S(1)}, u32[]{:S(2)}, u32[]{:S(2)}) collective-permute-start(f32[64,128]{1,0:T(8,128)S(1)} %log_add_fusion.7), channel_id=1, source_target_pairs={{0,64},{32,96},{64,128},{96,160},{128,192},{160,224},{192,0},{224,... | collective-permute-start | bytes 98312 | tf_op jit(solution)/shard_map/ppermute | solution.py:238
  115.2 4.6 %collective-permute-start.31 = (f32[64,128]{1,0:T(8,128)S(1)}, f32[64,128]{1,0:T(8,128)S(1)}, u32[]{:S(2)}, u32[]{:S(2)}) collective-permute-start(f32[64,128]{1,0:T(8,128)S(1)} %log_add_fusion.7), channel_id=1, source_target_pairs={{0,128},{32,160},{64,192},{96,224},{128,0},{160,32},{192,64},{224,... | collective-permute-start | bytes 98312 | tf_op jit(solution)/shard_map/ppermute | solution.py:238
  117.5 3.1 %collective-permute-start.32 = (f32[64,128]{1,0:T(8,128)S(1)}, f32[64,128]{1,0:T(8,128)S(1)}, u32[]{:S(2)}, u32[]{:S(2)}) collective-permute-start(f32[64,128]{1,0:T(8,128)S(1)} %log_add_fusion.7), channel_id=1, source_target_pairs={{0,192},{32,224},{64,0},{96,32},{128,64},{160,96},{192,128},{224,1... | collective-permute-start | bytes 98312 | tf_op jit(solution)/shard_map/ppermute | solution.py:238
  (7 other events, 54.7 us)

commit v2 on v1

--- a/solution.py
+++ b/solution.py
@@ -52,10 +52,7 @@
             right_ref[t] = wide_ref[t * 16 : (t + 1) * 16, :].astype(jnp.bfloat16)
 
 
-def squares(sub_coords, lane_coords, sub_ids_ref, lane_ids_ref, rows_ref, wide_ref, left_ref, right_ref, out_ref):
-    features(sub_coords, rows_ref, wide_ref, left_ref, None)
-    features(lane_coords, rows_ref, wide_ref, None, right_ref)
-
+def squares(sub_ids_ref, lane_ids_ref, left_ref, right_ref, out_ref):
     def some(g, carry):
         for u in range(GROUP):
             k = g * GROUP + u
@@ -128,13 +125,16 @@
     for copy in copies:
         copy.wait()
     make_table(table)
-    squares(tgt_coords, src_coords, tgt_ids, src_ids, rows, wide, left, right, square)
+    features(tgt_coords, rows, wide, left, None)
+    features(src_coords, rows, wide, None, right)
+    squares(tgt_ids, src_ids, left, right, square)
     half_step(start[...], src_ids, tgt_ids, count, square, table, columns, slots, tops, sums, out)
     put_total(out, mass[...])
 
 
-def square_kernel(sub_ids, lane_ids, sub_coords, lane_coords, square, rows, wide, left, right):
-    squares(sub_coords, lane_coords, sub_ids, lane_ids, rows, wide, left, right, square)
+def feature_kernel(sub_coords, lane_coords, left, right, rows, wide):
+    features(sub_coords, rows, wide, left, None)
+    features(lane_coords, rows, wide, None, right)
 
 
 def first_src_kernel(src_ids, tgt_ids, count, m0, m1, m2, m3, src_mass, square, table, out, tgt_const, columns, slots, tops, sums):
@@ -204,11 +204,19 @@
     )(*args)
 
 
-def square_call(sub_ids, lane_ids, sub_coords, lane_coords):
+def feature_call(sub_coords, lane_coords):
+    rows, wide, left, right = square_scratch(sub_coords.shape[1] // 128, lane_coords.shape[1] // 128)
     return pl.pallas_call(
-        square_kernel, out_shape=SQUARES, in_specs=[SMEM] * 2 + [VMEM] * 2, out_specs=VMEM,
-        scratch_shapes=square_scratch(sub_coords.shape[1] // 128, lane_coords.shape[1] // 128), compiler_params=PARAMS,
-    )(sub_ids, lane_ids, sub_coords, lane_coords)
+        feature_kernel,
+        out_shape=[jax.ShapeDtypeStruct(x.shape, x.dtype) for x in (left, right)],
+        in_specs=[VMEM] * 2, out_specs=[VMEM] * 2, scratch_shapes=[rows, wide], compiler_params=PARAMS,
+    )(sub_coords, lane_coords)
+
+
+def square_call(sub_ids, lane_ids, left, right):
+    return pl.pallas_call(
+        squares, out_shape=SQUARES, in_specs=[SMEM] * 2 + [VMEM] * 2, out_specs=VMEM, compiler_params=PARAMS,
+    )(sub_ids, lane_ids, left, right)
 
 
 def table_call():
@@ -238,13 +246,19 @@
     return lax.ppermute(value, "row", [(i, (i + 2 * shift) % 8) for i in range(8)])
 
 
-def over_col(message):
+def over_col(message, forms=None, lists=None):
     beside = col_permute(message, lambda y, z: (y, z ^ 1))
     corner = col_permute(message, lambda y, z: (y ^ 1, z ^ 1))
     above = col_permute(message, lambda y, z: (y ^ 1, z))
+    if forms is not None:
+        beside, corner, above, *forms = lax.optimization_barrier((beside, corner, above, *forms))
     merged = lse([message, beside, above, corner])
-    merged = lse([merged, col_permute(merged, lambda y, z: (y ^ 3, z))])
-    return [merged] + [col_permute(merged, lambda y, z, k=k: (y, z + k if z % 2 else z - k)) for k in (1, 3, -2)]
+    other = col_permute(merged, lambda y, z: (y ^ 3, z))
+    costs = None
+    if forms is not None:
+        other, costs = lax.optimization_barrier((other, square_call(*lists, *forms)))
+    merged = lse([merged, other])
+    return [merged] + [col_permute(merged, lambda y, z, k=k: (y, z + k if z % 2 else z - k)) for k in (1, 3, -2)], costs
 
 
 def over_row(message):
@@ -259,16 +273,17 @@
     tgt_mass = tgt_mass.reshape(64, 128)
     lists = (kept_src, kept_tgt, kept_count)
     message = first_call(*lists, tgt_start.reshape(64, 128), tgt_mass, src_coords, tgt_coords)
-    tgt_lanes = square_call(kept_src, kept_tgt, src_coords, tgt_coords)
     table = table_call()
-    src_lanes = square_call(kept_tgt, kept_src, tgt_coords, src_coords)
+    src_lanes = square_call(kept_tgt, kept_src, *feature_call(tgt_coords, src_coords))
     for iteration in range(ITERS):
-        parts = over_col(message)
         if iteration == 0:
+            parts, tgt_lanes = over_col(message, feature_call(src_coords, tgt_coords), (kept_src, kept_tgt))
             message, tgt_const = call(first_src_kernel, 64, [72, 8], *lists, *parts, src_mass, tgt_lanes, table)
         elif iteration + 1 < ITERS:
+            parts, _ = over_col(message)
             (message,) = call(src_kernel, 64, [64], *lists, *parts, src_mass, src_const, tgt_lanes, table)
         else:
+            parts, _ = over_col(message)
             message, src_potential = call(src_kernel, 64, [64, 128], *lists, *parts, src_mass, src_const, tgt_lanes, table)
         parts = over_row(message)
         if iteration == 0:

time: 122 us -> 120 us (0.984)
  starting transfers between devices: 59.6 us -> 55.6 us
  waiting for transfers between devices: 33.2 us -> 35.7 us
    ppermute x9, starting transfers between devices: 11.8 us -> 7.88 us  [row_permute(): lax.ppermute(value, 'row', [(i, (i + 2 * shift) % 8) for i in range(8)])]
    ppermute x9, waiting for transfers between devices: 5.37 us -> 8.93 us  [row_permute(): lax.ppermute(value, 'row', [(i, (i + 2 * shift) % 8) for i in range(8)])]
    pallas_call x2 -> x4, Pallas kernels: 4.69 us -> 4.66 us  [the longest x2 3.58 us: square_call(): pl.pallas_call(squares, out_shape=SQUARES, in_specs=[SMEM] * 2 + [VMEM] *...]
    unnamed x12 -> x16, local copies, waits for them, and re-layouts: 3.17 us -> 3.18 us
  transfers between devices with their start and end apart: 33 -> 33, of which waited for: 28 -> 24; matrix products, arithmetic and copies ran while one was open for 0% -> 0% of each run, Pallas kernels for 4% -> 4%
where the time goes in v2:
time: 120 us; the launch traced here: 119 us
  starting transfers between devices  55.6 us (46%)
  waiting for transfers between devices  35.7 us (30%)
  Pallas kernels  21.5 us (18%)
  local copies, waits for them, and re-layouts  3.18 us (3%)
  other arithmetic  1.96 us (2%)
  between operations  1.49 us (1%)
    ppermute x21, starting transfers between devices, col_permute(): return lax.ppermute(value, 'col', pairs)  33.8 us
    ppermute x21, waiting for transfers between devices, col_permute(): return lax.ppermute(value, 'col', pairs)  24.2 us
    ppermute x3, starting transfers between devices, over_row(): other = lax.ppermute(message, 'row', [(i, i ^ 1) for i in range(8)])  13.9 us
    pallas_call x5, Pallas kernels, call(): pl.pallas_call(body, out_shape=[jax.ShapeDtypeStruct((rows, 128), F32) fo...  11.4 us
    ppermute x9, waiting for transfers between devices, row_permute(): lax.ppermute(value, 'row', [(i, (i + 2 * shift) % 8) for i in range(8)])  8.93 us
    ppermute x9, starting transfers between devices, row_permute(): lax.ppermute(value, 'row', [(i, (i + 2 * shift) % 8) for i in range(8)])  7.88 us
    pallas_call x1, Pallas kernels, first_call(): pl.pallas_call(first_kernel, out_shape=jax.ShapeDtypeStruct((136, 128), F...  5.26 us
    pallas_call x2, Pallas kernels, square_call(): pl.pallas_call(squares, out_shape=SQUARES, in_specs=[SMEM] * 2 + [VMEM] *...  3.58 us
  transfers between devices with their start and end apart: 33, of which 24 were waited for; matrix products, arithmetic and copies ran while one was open for 0% of the time, Pallas kernels for 4%

profile of v2, /device:TPU:1, one launch (start us, length us, event | category | flops | bytes accessed | tf_op | source)
XLA Modules:
  0.0 119.4 jit_solution(6076539593788580746)
XLA Ops:
  1.3 5.3 %shard_map.95 = f32[136,128]{1,0:T(8,128)} custom-call(s32[1,1,64]{2,1,0:T(1,128)} %src_ids.9, s32[1,1,64]{2,1,0:T(1,128)} %tgt_ids.9, s32[1,1]{1,0:T(1,128)S(6)} %copy.10.count_list.count, f32[64,128]{1,0:T(8,128)} %bitcast.15, s32[64,128]{1,0:T(8,128)} %bitcast.12, s32[3,16384]{1,0:T(4,128)} %lane_coords.3, s32[3,8192]{1,0:T(4,128)} %sub_coords.3), custom_call_target="tpu_custom_call" | custom-call | tf_op jit(solution)/shard_map/pallas_call | solution.py:195
  6.6 2.2 %collective-permute-start.2 = (f32[136,128]{1,0:T(8,128)}, f32[136,128]{1,0:T(8,128)S(1)}, u32[]{:S(2)}, u32[]{:S(2)}) collective-permute-start(f32[136,128]{1,0:T(8,128)} %shard_map.95), channel_id=1, source_target_pairs={{8,0},{9,1},{10,2},{11,3},{12,4},{13,5},{14,6},{15,7},{0,8},{1,9},... | collective-permute-start | bytes 208904 | tf_op jit(solution)/shard_map/ppermute | solution.py:242
  8.8 1.5 %collective-permute-start.1 = (f32[136,128]{1,0:T(8,128)}, f32[136,128]{1,0:T(8,128)S(1)}, u32[]{:S(2)}, u32[]{:S(2)}) collective-permute-start(f32[136,128]{1,0:T(8,128)} %shard_map.95), channel_id=1, source_target_pairs={{9,0},{8,1},{11,2},{10,3},{13,4},{12,5},{15,6},{14,7},{1,8},{0,9},... | collective-permute-start | bytes 208904 | tf_op jit(solution)/shard_map/ppermute | solution.py:242
  14.9 3.3 %collective-permute-start.3 = (f32[136,128]{1,0:T(8,128)S(1)}, f32[136,128]{1,0:T(8,128)S(1)}, u32[]{:S(2)}, u32[]{:S(2)}) collective-permute-start(f32[136,128]{1,0:T(8,128)S(1)} %log_add_fusion.1), channel_id=1, source_target_pairs={{24,0},{25,1},{26,2},{27,3},{28,4},{29,5},{30,6},{31,7},{16,8},{17... | collective-permute-start | bytes 208904 | tf_op jit(solution)/shard_map/ppermute | solution.py:242
  19.5 1.8 %shard_map.97.square = f32[64,128,128]{2,1,0:T(8,128)S(1)} custom-call(s32[1,1,64]{2,1,0:T(1,128)S(1)} %copy-done.6, s32[1,1,64]{2,1,0:T(1,128)S(1)} %copy-done.7, bf16[16,128,128]{2,1,0:T(8,128)(2,1)S(1)} %get-tuple-element.24.left_ref, bf16[64,16,128]{2,1,0:T(8,128)(2,1)S(1)} %get-tuple-element.25.right_ref), custom_call_target="tpu_custom_call" | custom-call | tf_op jit(solution)/shard_map/pallas_call | solution.py:217
  21.4 4.7 %collective-permute-start.6 = (f32[136,128]{1,0:T(8,128)S(1)}, f32[136,128]{1,0:T(8,128)S(1)}, u32[]{:S(2)}, u32[]{:S(2)}) collective-permute-start(f32[136,128]{1,0:T(8,128)S(1)} %log_add_fusion.m0), channel_id=1, source_target_pairs={{2,0},{7,1},{4,2},{1,3},{6,4},{3,5},{0,6},{5,7},{10,8},{15,9},{12,... | collective-permute-start | bytes 208904 | tf_op jit(solution)/shard_map/ppermute | solution.py:242
  26.1 1.6 %collective-permute-start.5 = (f32[136,128]{1,0:T(8,128)S(1)}, f32[136,128]{1,0:T(8,128)S(1)}, u32[]{:S(2)}, u32[]{:S(2)}) collective-permute-start(f32[136,128]{1,0:T(8,128)S(1)} %log_add_fusion.m0), channel_id=1, source_target_pairs={{5,0},{4,1},{7,2},{6,3},{1,4},{0,5},{3,6},{2,7},{13,8},{12,9},{15,... | collective-permute-start | bytes 208904 | tf_op jit(solution)/shard_map/ppermute | solution.py:242
  27.9 5.8 %collective-permute-done.5.m2 = f32[136,128]{1,0:T(8,128)S(1)} collective-permute-done((f32[136,128]{1,0:T(8,128)S(1)}, f32[136,128]{1,0:T(8,128)S(1)}, u32[]{:S(2)}, u32[]{:S(2)}) %collective-permute-start.5) | collective-permute-done | bytes 69664 | tf_op jit(solution)/shard_map/ppermute | solution.py:242
  33.8 2.2 %shard_map.99 = (f32[72,128]{1,0:T(8,128)S(1)}, f32[8,128]{1,0:T(8,128)S(1)}) custom-call(s32[1,1,64]{2,1,0:T(1,128)S(1)} %copy-done.6, s32[1,1,64]{2,1,0:T(1,128)S(1)} %copy-done.7, s32[1,1]{1,0:T(1,128)S(6)} %copy.10.count_list.count, f32[136,128]{1,0:T(8,128)S(1)} %log_add_fusion.m0, f32[136,128]{1,0:T(8,128)S(1)} %collective-permute-done.4.m1, ...), custom_call_target="tpu_custom_call" | custom-call | tf_op jit(solution)/shard_map/pallas_call | solution.py:227
  36.0 3.2 %collective-permute-start.7 = (f32[72,128]{1,0:T(8,128)S(1)}, f32[72,128]{1,0:T(8,128)S(1)}, u32[]{:S(2)}, u32[]{:S(2)}) collective-permute-start(f32[72,128]{1,0:T(8,128)S(1)} %get-tuple-element.28), channel_id=1, source_target_pairs={{0,32},{32,0},{64,96},{96,64},{128,160},{160,128},{192,224},{224,1... | collective-permute-start | bytes 110600 | tf_op jit(solution)/shard_map/ppermute | solution.py:265
  40.0 2.6 %collective-permute-start.10 = (f32[72,128]{1,0:T(8,128)S(1)}, f32[72,128]{1,0:T(8,128)S(1)}, u32[]{:S(2)}, u32[]{:S(2)}) collective-permute-start(f32[72,128]{1,0:T(8,128)S(1)} %log_add_fusion.6.m0), channel_id=1, source_target_pairs={{0,192},{32,224},{64,0},{96,32},{128,64},{160,96},{192,128},{224,1... | collective-permute-start | bytes 110600 | tf_op jit(solution)/shard_map/ppermute | solution.py:246
  44.2 1.8 %shard_map.101.square = f32[64,128,128]{2,1,0:T(8,128)S(1)} custom-call(s32[1,1,64]{2,1,0:T(1,128)S(1)} %copy-done.7, s32[1,1,64]{2,1,0:T(1,128)S(1)} %copy-done.6, bf16[8,128,128]{2,1,0:T(8,128)(2,1)S(1)} %get-tuple-element.30.left_ref, bf16[128,16,128]{2,1,0:T(8,128)(2,1)S(1)} %get-tuple-element.31.right_ref), custom_call_target="tpu_custom_call" | custom-call | tf_op jit(solution)/shard_map/pallas_call | solution.py:217
  47.3 2.2 %shard_map.102 = (f32[128,128]{1,0:T(8,128)S(1)}, f32[8,128]{1,0:T(8,128)S(1)}) custom-call(s32[1,1,64]{2,1,0:T(1,128)S(1)} %copy-done.6, s32[1,1,64]{2,1,0:T(1,128)S(1)} %copy-done.7, s32[1,1]{1,0:T(1,128)S(6)} %copy.10.count_list.count, f32[72,128]{1,0:T(8,128)S(1)} %log_add_fusion.6.m0, f32[72,128]{1,0:T(8,128)S(1)} %collective-permute-done.8.m1, ...), custom_call_target="tpu_custom_call" | custom-call | tf_op jit(solution)/shard_map/pallas_call | solution.py:227
  49.8 2.4 %collective-permute-start.11 = (f32[128,128]{1,0:T(8,128)S(1)}, f32[128,128]{1,0:T(8,128)S(1)}, u32[]{:S(2)}, u32[]{:S(2)}) collective-permute-start(f32[128,128]{1,0:T(8,128)S(1)} %get-tuple-element.32), channel_id=1, source_target_pairs={{1,0},{0,1},{3,2},{2,3},{5,4},{4,5},{7,6},{6,7},{9,8},{8,9},{11,10... | collective-permute-start | bytes 196616 | tf_op jit(solution)/shard_map/ppermute | solution.py:242
  54.0 3.0 %collective-permute-start.14 = (f32[128,128]{1,0:T(8,128)S(1)}, f32[128,128]{1,0:T(8,128)S(1)}, u32[]{:S(2)}, u32[]{:S(2)}) collective-permute-start(f32[128,128]{1,0:T(8,128)S(1)} %log_add_fusion.5), channel_id=1, source_target_pairs={{24,0},{25,1},{26,2},{27,3},{28,4},{29,5},{30,6},{31,7},{16,8},{17... | collective-permute-start | bytes 196616 | tf_op jit(solution)/shard_map/ppermute | solution.py:242
  57.0 1.7 %collective-permute-done.14 = f32[128,128]{1,0:T(8,128)S(1)} collective-permute-done((f32[128,128]{1,0:T(8,128)S(1)}, f32[128,128]{1,0:T(8,128)S(1)}, u32[]{:S(2)}, u32[]{:S(2)}) %collective-permute-start.14) | collective-permute-done | bytes 65568 | tf_op jit(solution)/shard_map/ppermute | solution.py:242
  58.7 1.5 %collective-permute-start.17 = (f32[128,128]{1,0:T(8,128)S(1)}, f32[128,128]{1,0:T(8,128)S(1)}, u32[]{:S(2)}, u32[]{:S(2)}) collective-permute-start(f32[128,128]{1,0:T(8,128)S(1)} %log_add_fusion.4.m0), channel_id=1, source_target_pairs={{2,0},{7,1},{4,2},{1,3},{6,4},{3,5},{0,6},{5,7},{10,8},{15,9},{12,... | collective-permute-start | bytes 196616 | tf_op jit(solution)/shard_map/ppermute | solution.py:242
  60.2 2.0 %collective-permute-start.16 = (f32[128,128]{1,0:T(8,128)S(1)}, f32[128,128]{1,0:T(8,128)S(1)}, u32[]{:S(2)}, u32[]{:S(2)}) collective-permute-start(f32[128,128]{1,0:T(8,128)S(1)} %log_add_fusion.4.m0), channel_id=1, source_target_pairs={{5,0},{4,1},{7,2},{6,3},{1,4},{0,5},{3,6},{2,7},{13,8},{12,9},{15,... | collective-permute-start | bytes 196616 | tf_op jit(solution)/shard_map/ppermute | solution.py:242
  63.5 2.8 %collective-permute-done.16.m2 = f32[128,128]{1,0:T(8,128)S(1)} collective-permute-done((f32[128,128]{1,0:T(8,128)S(1)}, f32[128,128]{1,0:T(8,128)S(1)}, u32[]{:S(2)}, u32[]{:S(2)}) %collective-permute-start.16) | collective-permute-done | bytes 65568 | tf_op jit(solution)/shard_map/ppermute | solution.py:242
  67.1 2.2 %shard_map.103 = f32[64,128]{1,0:T(8,128)S(1)} custom-call(s32[1,1,64]{2,1,0:T(1,128)S(1)} %copy-done.6, s32[1,1,64]{2,1,0:T(1,128)S(1)} %copy-done.7, s32[1,1]{1,0:T(1,128)S(6)} %copy.10.count_list.count, f32[128,128]{1,0:T(8,128)S(1)} %log_add_fusion.4.m0, f32[128,128]{1,0:T(8,128)S(1)} %collective-permute-done.15.m1, ...), custom_call_target="tpu_custom_call" | custom-call | tf_op jit(solution)/shard_map/pallas_call | solution.py:227
  69.3 5.8 %collective-permute-start.18 = (f32[64,128]{1,0:T(8,128)S(1)}, f32[64,128]{1,0:T(8,128)S(1)}, u32[]{:S(2)}, u32[]{:S(2)}) collective-permute-start(f32[64,128]{1,0:T(8,128)S(1)} %shard_map.103), channel_id=1, source_target_pairs={{0,32},{32,0},{64,96},{96,64},{128,160},{160,128},{192,224},{224,1... | collective-permute-start | bytes 98312 | tf_op jit(solution)/shard_map/ppermute | solution.py:265
  78.9 1.7 %collective-permute-done.20.m2 = f32[64,128]{1,0:T(8,128)S(1)} collective-permute-done((f32[64,128]{1,0:T(8,128)S(1)}, f32[64,128]{1,0:T(8,128)S(1)}, u32[]{:S(2)}, u32[]{:S(2)}) %collective-permute-start.20) | collective-permute-done | bytes 32800 | tf_op jit(solution)/shard_map/ppermute | solution.py:246
  81.9 2.2 %shard_map.104 = f32[128,128]{1,0:T(8,128)S(1)} custom-call(s32[1,1,64]{2,1,0:T(1,128)S(1)} %copy-done.6, s32[1,1,64]{2,1,0:T(1,128)S(1)} %copy-done.7, s32[1,1]{1,0:T(1,128)S(6)} %copy.10.count_list.count, f32[64,128]{1,0:T(8,128)S(1)} %log_add_fusion.8.m0, f32[64,128]{1,0:T(8,128)S(1)} %collective-permute-done.19.m1, ...), custom_call_target="tpu_custom_call" | custom-call | tf_op jit(solution)/shard_map/pallas_call | solution.py:227
  84.2 2.1 %collective-permute-start.23 = (f32[128,128]{1,0:T(8,128)S(1)}, f32[128,128]{1,0:T(8,128)S(1)}, u32[]{:S(2)}, u32[]{:S(2)}) collective-permute-start(f32[128,128]{1,0:T(8,128)S(1)} %shard_map.104), channel_id=1, source_target_pairs={{8,0},{9,1},{10,2},{11,3},{12,4},{13,5},{14,6},{15,7},{0,8},{1,9},... | collective-permute-start | bytes 196616 | tf_op jit(solution)/shard_map/ppermute | solution.py:242
  89.8 2.2 %collective-permute-start.25 = (f32[128,128]{1,0:T(8,128)S(1)}, f32[128,128]{1,0:T(8,128)S(1)}, u32[]{:S(2)}, u32[]{:S(2)}) collective-permute-start(f32[128,128]{1,0:T(8,128)S(1)} %log_add_fusion.3), channel_id=1, source_target_pairs={{24,0},{25,1},{26,2},{27,3},{28,4},{29,5},{30,6},{31,7},{16,8},{17... | collective-permute-start | bytes 196616 | tf_op jit(solution)/shard_map/ppermute | solution.py:242
  92.0 2.2 %collective-permute-done.25 = f32[128,128]{1,0:T(8,128)S(1)} collective-permute-done((f32[128,128]{1,0:T(8,128)S(1)}, f32[128,128]{1,0:T(8,128)S(1)}, u32[]{:S(2)}, u32[]{:S(2)}) %collective-permute-start.25) | collective-permute-done | bytes 65568 | tf_op jit(solution)/shard_map/ppermute | solution.py:242
  94.3 2.7 %collective-permute-start.28 = (f32[128,128]{1,0:T(8,128)S(1)}, f32[128,128]{1,0:T(8,128)S(1)}, u32[]{:S(2)}, u32[]{:S(2)}) collective-permute-start(f32[128,128]{1,0:T(8,128)S(1)} %log_add_fusion.2.m0), channel_id=1, source_target_pairs={{2,0},{7,1},{4,2},{1,3},{6,4},{3,5},{0,6},{5,7},{10,8},{15,9},{12,... | collective-permute-start | bytes 196616 | tf_op jit(solution)/shard_map/ppermute | solution.py:242
  97.6 1.5 %collective-permute-start.26 = (f32[128,128]{1,0:T(8,128)S(1)}, f32[128,128]{1,0:T(8,128)S(1)}, u32[]{:S(2)}, u32[]{:S(2)}) collective-permute-start(f32[128,128]{1,0:T(8,128)S(1)} %log_add_fusion.2.m0), channel_id=1, source_target_pairs={{7,0},{2,1},{1,2},{4,3},{3,4},{6,5},{5,6},{0,7},{15,8},{10,9},{9,1... | collective-permute-start | bytes 196616 | tf_op jit(solution)/shard_map/ppermute | solution.py:242
  99.1 5.3 %collective-permute-done.27.m2 = f32[128,128]{1,0:T(8,128)S(1)} collective-permute-done((f32[128,128]{1,0:T(8,128)S(1)}, f32[128,128]{1,0:T(8,128)S(1)}, u32[]{:S(2)}, u32[]{:S(2)}) %collective-permute-start.27) | collective-permute-done | bytes 65568 | tf_op jit(solution)/shard_map/ppermute | solution.py:242
  104.4 2.7 %shard_map.105 = (f32[64,128]{1,0:T(8,128)S(1)}, f32[128,128]{1,0:T(8,128)}) custom-call(s32[1,1,64]{2,1,0:T(1,128)S(1)} %copy-done.6, s32[1,1,64]{2,1,0:T(1,128)S(1)} %copy-done.7, s32[1,1]{1,0:T(1,128)S(6)} %copy.10.count_list.count, f32[128,128]{1,0:T(8,128)S(1)} %log_add_fusion.2.m0, f32[128,128]{1,0:T(8,128)S(1)} %collective-permute-done.26.m1, ...), custom_call_target="tpu_custom_call" | custom-call | tf_op jit(solution)/shard_map/pallas_call | solution.py:227
  107.1 4.9 %collective-permute-start.29 = (f32[64,128]{1,0:T(8,128)S(1)}, f32[64,128]{1,0:T(8,128)S(1)}, u32[]{:S(2)}, u32[]{:S(2)}) collective-permute-start(f32[64,128]{1,0:T(8,128)S(1)} %get-tuple-element.35), channel_id=1, source_target_pairs={{0,32},{32,0},{64,96},{96,64},{128,160},{160,128},{192,224},{224,1... | collective-permute-start | bytes 98312 | tf_op jit(solution)/shard_map/ppermute | solution.py:265
  115.7 2.8 %collective-permute-done.31 = f32[64,128]{1,0:T(8,128)S(1)} collective-permute-done((f32[64,128]{1,0:T(8,128)S(1)}, f32[64,128]{1,0:T(8,128)S(1)}, u32[]{:S(2)}, u32[]{:S(2)}) %collective-permute-start.31) | collective-permute-done | bytes 32800 | tf_op jit(solution)/shard_map/ppermute | solution.py:246
  (72 shorter events, 28.3 us)
Async XLA Ops:
  6.6 6.3 %collective-permute-start.2 = (f32[136,128]{1,0:T(8,128)}, f32[136,128]{1,0:T(8,128)S(1)}, u32[]{:S(2)}, u32[]{:S(2)}) collective-permute-start(f32[136,128]{1,0:T(8,128)} %shard_map.95), channel_id=1, source_target_pairs={{8,0},{9,1},{10,2},{11,3},{12,4},{13,5},{14,6},{15,7},{0,8},{1,9},... | collective-permute-start | bytes 208904 | tf_op jit(solution)/shard_map/ppermute | solution.py:242
  8.8 4.3 %collective-permute-start.1 = (f32[136,128]{1,0:T(8,128)}, f32[136,128]{1,0:T(8,128)S(1)}, u32[]{:S(2)}, u32[]{:S(2)}) collective-permute-start(f32[136,128]{1,0:T(8,128)} %shard_map.95), channel_id=1, source_target_pairs={{9,0},{8,1},{11,2},{10,3},{13,4},{12,5},{15,6},{14,7},{1,8},{0,9},... | collective-permute-start | bytes 208904 | tf_op jit(solution)/shard_map/ppermute | solution.py:242
  10.3 3.7 %collective-permute-start = (f32[136,128]{1,0:T(8,128)}, f32[136,128]{1,0:T(8,128)S(1)}, u32[]{:S(2)}, u32[]{:S(2)}) collective-permute-start(f32[136,128]{1,0:T(8,128)} %shard_map.95), channel_id=1, source_target_pairs={{1,0},{0,1},{3,2},{2,3},{5,4},{4,5},{7,6},{6,7},{9,8},{8,9},{11,10... | collective-permute-start | bytes 208904 | tf_op jit(solution)/shard_map/ppermute | solution.py:242
  14.9 6.4 %collective-permute-start.3 = (f32[136,128]{1,0:T(8,128)S(1)}, f32[136,128]{1,0:T(8,128)S(1)}, u32[]{:S(2)}, u32[]{:S(2)}) collective-permute-start(f32[136,128]{1,0:T(8,128)S(1)} %log_add_fusion.1), channel_id=1, source_target_pairs={{24,0},{25,1},{26,2},{27,3},{28,4},{29,5},{30,6},{31,7},{16,8},{17... | collective-permute-start | bytes 208904 | tf_op jit(solution)/shard_map/ppermute | solution.py:242
  21.4 6.5 %collective-permute-start.6 = (f32[136,128]{1,0:T(8,128)S(1)}, f32[136,128]{1,0:T(8,128)S(1)}, u32[]{:S(2)}, u32[]{:S(2)}) collective-permute-start(f32[136,128]{1,0:T(8,128)S(1)} %log_add_fusion.m0), channel_id=1, source_target_pairs={{2,0},{7,1},{4,2},{1,3},{6,4},{3,5},{0,6},{5,7},{10,8},{15,9},{12,... | collective-permute-start | bytes 208904 | tf_op jit(solution)/shard_map/ppermute | solution.py:242
  26.1 7.6 %collective-permute-start.5 = (f32[136,128]{1,0:T(8,128)S(1)}, f32[136,128]{1,0:T(8,128)S(1)}, u32[]{:S(2)}, u32[]{:S(2)}) collective-permute-start(f32[136,128]{1,0:T(8,128)S(1)} %log_add_fusion.m0), channel_id=1, source_target_pairs={{5,0},{4,1},{7,2},{6,3},{1,4},{0,5},{3,6},{2,7},{13,8},{12,9},{15,... | collective-permute-start | bytes 208904 | tf_op jit(solution)/shard_map/ppermute | solution.py:242
  27.8 6.0 %collective-permute-start.4 = (f32[136,128]{1,0:T(8,128)S(1)}, f32[136,128]{1,0:T(8,128)S(1)}, u32[]{:S(2)}, u32[]{:S(2)}) collective-permute-start(f32[136,128]{1,0:T(8,128)S(1)} %log_add_fusion.m0), channel_id=1, source_target_pairs={{7,0},{2,1},{1,2},{4,3},{3,4},{6,5},{5,6},{0,7},{15,8},{10,9},{9,1... | collective-permute-start | bytes 208904 | tf_op jit(solution)/shard_map/ppermute | solution.py:242
  36.0 4.0 %collective-permute-start.7 = (f32[72,128]{1,0:T(8,128)S(1)}, f32[72,128]{1,0:T(8,128)S(1)}, u32[]{:S(2)}, u32[]{:S(2)}) collective-permute-start(f32[72,128]{1,0:T(8,128)S(1)} %get-tuple-element.28), channel_id=1, source_target_pairs={{0,32},{32,0},{64,96},{96,64},{128,160},{160,128},{192,224},{224,1... | collective-permute-start | bytes 110600 | tf_op jit(solution)/shard_map/ppermute | solution.py:265
  40.0 6.0 %collective-permute-start.10 = (f32[72,128]{1,0:T(8,128)S(1)}, f32[72,128]{1,0:T(8,128)S(1)}, u32[]{:S(2)}, u32[]{:S(2)}) collective-permute-start(f32[72,128]{1,0:T(8,128)S(1)} %log_add_fusion.6.m0), channel_id=1, source_target_pairs={{0,192},{32,224},{64,0},{96,32},{128,64},{160,96},{192,128},{224,1... | collective-permute-start | bytes 110600 | tf_op jit(solution)/shard_map/ppermute | solution.py:246
  42.6 4.3 %collective-permute-start.9 = (f32[72,128]{1,0:T(8,128)S(1)}, f32[72,128]{1,0:T(8,128)S(1)}, u32[]{:S(2)}, u32[]{:S(2)}) collective-permute-start(f32[72,128]{1,0:T(8,128)S(1)} %log_add_fusion.6.m0), channel_id=1, source_target_pairs={{0,128},{32,160},{64,192},{96,224},{128,0},{160,32},{192,64},{224,... | collective-permute-start | bytes 110600 | tf_op jit(solution)/shard_map/ppermute | solution.py:246
  43.1 4.2 %collective-permute-start.8 = (f32[72,128]{1,0:T(8,128)S(1)}, f32[72,128]{1,0:T(8,128)S(1)}, u32[]{:S(2)}, u32[]{:S(2)}) collective-permute-start(f32[72,128]{1,0:T(8,128)S(1)} %log_add_fusion.6.m0), channel_id=1, source_target_pairs={{0,64},{32,96},{64,128},{96,160},{128,192},{160,224},{192,0},{224,... | collective-permute-start | bytes 110600 | tf_op jit(solution)/shard_map/ppermute | solution.py:246
  49.5 4.1 %collective-permute-start.13 = (f32[128,128]{1,0:T(8,128)S(1)}, f32[128,128]{1,0:T(8,128)S(1)}, u32[]{:S(2)}, u32[]{:S(2)}) collective-permute-start(f32[128,128]{1,0:T(8,128)S(1)} %get-tuple-element.32), channel_id=1, source_target_pairs={{9,0},{8,1},{11,2},{10,3},{13,4},{12,5},{15,6},{14,7},{1,8},{0,9},... | collective-permute-start | bytes 196616 | tf_op jit(solution)/shard_map/ppermute | solution.py:242
  49.6 4.0 %collective-permute-start.12 = (f32[128,128]{1,0:T(8,128)S(1)}, f32[128,128]{1,0:T(8,128)S(1)}, u32[]{:S(2)}, u32[]{:S(2)}) collective-permute-start(f32[128,128]{1,0:T(8,128)S(1)} %get-tuple-element.32), channel_id=1, source_target_pairs={{8,0},{9,1},{10,2},{11,3},{12,4},{13,5},{14,6},{15,7},{0,8},{1,9},... | collective-permute-start | bytes 196616 | tf_op jit(solution)/shard_map/ppermute | solution.py:242
  49.8 4.1 %collective-permute-start.11 = (f32[128,128]{1,0:T(8,128)S(1)}, f32[128,128]{1,0:T(8,128)S(1)}, u32[]{:S(2)}, u32[]{:S(2)}) collective-permute-start(f32[128,128]{1,0:T(8,128)S(1)} %get-tuple-element.32), channel_id=1, source_target_pairs={{1,0},{0,1},{3,2},{2,3},{5,4},{4,5},{7,6},{6,7},{9,8},{8,9},{11,10... | collective-permute-start | bytes 196616 | tf_op jit(solution)/shard_map/ppermute | solution.py:242
  54.0 4.7 %collective-permute-start.14 = (f32[128,128]{1,0:T(8,128)S(1)}, f32[128,128]{1,0:T(8,128)S(1)}, u32[]{:S(2)}, u32[]{:S(2)}) collective-permute-start(f32[128,128]{1,0:T(8,128)S(1)} %log_add_fusion.5), channel_id=1, source_target_pairs={{24,0},{25,1},{26,2},{27,3},{28,4},{29,5},{30,6},{31,7},{16,8},{17... | collective-permute-start | bytes 196616 | tf_op jit(solution)/shard_map/ppermute | solution.py:242
  58.7 4.8 %collective-permute-start.17 = (f32[128,128]{1,0:T(8,128)S(1)}, f32[128,128]{1,0:T(8,128)S(1)}, u32[]{:S(2)}, u32[]{:S(2)}) collective-permute-start(f32[128,128]{1,0:T(8,128)S(1)} %log_add_fusion.4.m0), channel_id=1, source_target_pairs={{2,0},{7,1},{4,2},{1,3},{6,4},{3,5},{0,6},{5,7},{10,8},{15,9},{12,... | collective-permute-start | bytes 196616 | tf_op jit(solution)/shard_map/ppermute | solution.py:242
  60.2 6.2 %collective-permute-start.16 = (f32[128,128]{1,0:T(8,128)S(1)}, f32[128,128]{1,0:T(8,128)S(1)}, u32[]{:S(2)}, u32[]{:S(2)}) collective-permute-start(f32[128,128]{1,0:T(8,128)S(1)} %log_add_fusion.4.m0), channel_id=1, source_target_pairs={{5,0},{4,1},{7,2},{6,3},{1,4},{0,5},{3,6},{2,7},{13,8},{12,9},{15,... | collective-permute-start | bytes 196616 | tf_op jit(solution)/shard_map/ppermute | solution.py:242
  62.2 5.0 %collective-permute-start.15 = (f32[128,128]{1,0:T(8,128)S(1)}, f32[128,128]{1,0:T(8,128)S(1)}, u32[]{:S(2)}, u32[]{:S(2)}) collective-permute-start(f32[128,128]{1,0:T(8,128)S(1)} %log_add_fusion.4.m0), channel_id=1, source_target_pairs={{7,0},{2,1},{1,2},{4,3},{3,4},{6,5},{5,6},{0,7},{15,8},{10,9},{9,1... | collective-permute-start | bytes 196616 | tf_op jit(solution)/shard_map/ppermute | solution.py:242
  69.3 6.7 %collective-permute-start.18 = (f32[64,128]{1,0:T(8,128)S(1)}, f32[64,128]{1,0:T(8,128)S(1)}, u32[]{:S(2)}, u32[]{:S(2)}) collective-permute-start(f32[64,128]{1,0:T(8,128)S(1)} %shard_map.103), channel_id=1, source_target_pairs={{0,32},{32,0},{64,96},{96,64},{128,160},{160,128},{192,224},{224,1... | collective-permute-start | bytes 98312 | tf_op jit(solution)/shard_map/ppermute | solution.py:265
  76.0 2.8 %collective-permute-start.21 = (f32[64,128]{1,0:T(8,128)S(1)}, f32[64,128]{1,0:T(8,128)S(1)}, u32[]{:S(2)}, u32[]{:S(2)}) collective-permute-start(f32[64,128]{1,0:T(8,128)S(1)} %log_add_fusion.8.m0), channel_id=1, source_target_pairs={{0,192},{32,224},{64,0},{96,32},{128,64},{160,96},{192,128},{224,1... | collective-permute-start | bytes 98312 | tf_op jit(solution)/shard_map/ppermute | solution.py:246
  76.3 4.3 %collective-permute-start.20 = (f32[64,128]{1,0:T(8,128)S(1)}, f32[64,128]{1,0:T(8,128)S(1)}, u32[]{:S(2)}, u32[]{:S(2)}) collective-permute-start(f32[64,128]{1,0:T(8,128)S(1)} %log_add_fusion.8.m0), channel_id=1, source_target_pairs={{0,128},{32,160},{64,192},{96,224},{128,0},{160,32},{192,64},{224,... | collective-permute-start | bytes 98312 | tf_op jit(solution)/shard_map/ppermute | solution.py:246
  77.5 4.4 %collective-permute-start.19 = (f32[64,128]{1,0:T(8,128)S(1)}, f32[64,128]{1,0:T(8,128)S(1)}, u32[]{:S(2)}, u32[]{:S(2)}) collective-permute-start(f32[64,128]{1,0:T(8,128)S(1)} %log_add_fusion.8.m0), channel_id=1, source_target_pairs={{0,64},{32,96},{64,128},{96,160},{128,192},{160,224},{192,0},{224,... | collective-permute-start | bytes 98312 | tf_op jit(solution)/shard_map/ppermute | solution.py:246
  84.1 4.2 %collective-permute-start.24 = (f32[128,128]{1,0:T(8,128)S(1)}, f32[128,128]{1,0:T(8,128)S(1)}, u32[]{:S(2)}, u32[]{:S(2)}) collective-permute-start(f32[128,128]{1,0:T(8,128)S(1)} %shard_map.104), channel_id=1, source_target_pairs={{9,0},{8,1},{11,2},{10,3},{13,4},{12,5},{15,6},{14,7},{1,8},{0,9},... | collective-permute-start | bytes 196616 | tf_op jit(solution)/shard_map/ppermute | solution.py:242
  84.2 4.4 %collective-permute-start.23 = (f32[128,128]{1,0:T(8,128)S(1)}, f32[128,128]{1,0:T(8,128)S(1)}, u32[]{:S(2)}, u32[]{:S(2)}) collective-permute-start(f32[128,128]{1,0:T(8,128)S(1)} %shard_map.104), channel_id=1, source_target_pairs={{8,0},{9,1},{10,2},{11,3},{12,4},{13,5},{14,6},{15,7},{0,8},{1,9},... | collective-permute-start | bytes 196616 | tf_op jit(solution)/shard_map/ppermute | solution.py:242
  86.3 3.4 %collective-permute-start.22 = (f32[128,128]{1,0:T(8,128)S(1)}, f32[128,128]{1,0:T(8,128)S(1)}, u32[]{:S(2)}, u32[]{:S(2)}) collective-permute-start(f32[128,128]{1,0:T(8,128)S(1)} %shard_map.104), channel_id=1, source_target_pairs={{1,0},{0,1},{3,2},{2,3},{5,4},{4,5},{7,6},{6,7},{9,8},{8,9},{11,10... | collective-permute-start | bytes 196616 | tf_op jit(solution)/shard_map/ppermute | solution.py:242
  89.8 4.4 %collective-permute-start.25 = (f32[128,128]{1,0:T(8,128)S(1)}, f32[128,128]{1,0:T(8,128)S(1)}, u32[]{:S(2)}, u32[]{:S(2)}) collective-permute-start(f32[128,128]{1,0:T(8,128)S(1)} %log_add_fusion.3), channel_id=1, source_target_pairs={{24,0},{25,1},{26,2},{27,3},{28,4},{29,5},{30,6},{31,7},{16,8},{17... | collective-permute-start | bytes 196616 | tf_op jit(solution)/shard_map/ppermute | solution.py:242
  94.3 4.8 %collective-permute-start.28 = (f32[128,128]{1,0:T(8,128)S(1)}, f32[128,128]{1,0:T(8,128)S(1)}, u32[]{:S(2)}, u32[]{:S(2)}) collective-permute-start(f32[128,128]{1,0:T(8,128)S(1)} %log_add_fusion.2.m0), channel_id=1, source_target_pairs={{2,0},{7,1},{4,2},{1,3},{6,4},{3,5},{0,6},{5,7},{10,8},{15,9},{12,... | collective-permute-start | bytes 196616 | tf_op jit(solution)/shard_map/ppermute | solution.py:242
  96.9 7.5 %collective-permute-start.27 = (f32[128,128]{1,0:T(8,128)S(1)}, f32[128,128]{1,0:T(8,128)S(1)}, u32[]{:S(2)}, u32[]{:S(2)}) collective-permute-start(f32[128,128]{1,0:T(8,128)S(1)} %log_add_fusion.2.m0), channel_id=1, source_target_pairs={{5,0},{4,1},{7,2},{6,3},{1,4},{0,5},{3,6},{2,7},{13,8},{12,9},{15,... | collective-permute-start | bytes 196616 | tf_op jit(solution)/shard_map/ppermute | solution.py:242
  97.6 6.8 %collective-permute-start.26 = (f32[128,128]{1,0:T(8,128)S(1)}, f32[128,128]{1,0:T(8,128)S(1)}, u32[]{:S(2)}, u32[]{:S(2)}) collective-permute-start(f32[128,128]{1,0:T(8,128)S(1)} %log_add_fusion.2.m0), channel_id=1, source_target_pairs={{7,0},{2,1},{1,2},{4,3},{3,4},{6,5},{5,6},{0,7},{15,8},{10,9},{9,1... | collective-permute-start | bytes 196616 | tf_op jit(solution)/shard_map/ppermute | solution.py:242
  107.1 5.7 %collective-permute-start.29 = (f32[64,128]{1,0:T(8,128)S(1)}, f32[64,128]{1,0:T(8,128)S(1)}, u32[]{:S(2)}, u32[]{:S(2)}) collective-permute-start(f32[64,128]{1,0:T(8,128)S(1)} %get-tuple-element.35), channel_id=1, source_target_pairs={{0,32},{32,0},{64,96},{96,64},{128,160},{160,128},{192,224},{224,1... | collective-permute-start | bytes 98312 | tf_op jit(solution)/shard_map/ppermute | solution.py:265
  114.2 4.3 %collective-permute-start.31 = (f32[64,128]{1,0:T(8,128)S(1)}, f32[64,128]{1,0:T(8,128)S(1)}, u32[]{:S(2)}, u32[]{:S(2)}) collective-permute-start(f32[64,128]{1,0:T(8,128)S(1)} %log_add_fusion.7), channel_id=1, source_target_pairs={{0,128},{32,160},{64,192},{96,224},{128,0},{160,32},{192,64},{224,... | collective-permute-start | bytes 98312 | tf_op jit(solution)/shard_map/ppermute | solution.py:246
  114.8 4.0 %collective-permute-start.30 = (f32[64,128]{1,0:T(8,128)S(1)}, f32[64,128]{1,0:T(8,128)S(1)}, u32[]{:S(2)}, u32[]{:S(2)}) collective-permute-start(f32[64,128]{1,0:T(8,128)S(1)} %log_add_fusion.7), channel_id=1, source_target_pairs={{0,64},{32,96},{64,128},{96,160},{128,192},{160,224},{192,0},{224,... | collective-permute-start | bytes 98312 | tf_op jit(solution)/shard_map/ppermute | solution.py:246
  (9 other events, 97.4 us)

commit v3 on v2

--- a/solution.py
+++ b/solution.py
@@ -122,11 +122,13 @@
     copies = [pltpu.make_async_copy(here, there, sems.at[n]) for n, (here, there) in enumerate(pairs)]
     for copy in copies:
         copy.start()
-    for copy in copies:
+    make_table(table)
+    copies[6].wait()
+    features(tgt_coords, rows, wide, left, None)
+    copies[5].wait()
+    features(src_coords, rows, wide, None, right)
+    for copy in copies[:5]:
         copy.wait()
-    make_table(table)
-    features(tgt_coords, rows, wide, left, None)
-    features(src_coords, rows, wide, None, right)
     squares(tgt_ids, src_ids, left, right, square)
     half_step(start[...], src_ids, tgt_ids, count, square, table, columns, slots, tops, sums, out)
     put_total(out, mass[...])

time: 120 us -> 120 us (level)
  no operation moved by 1% of the time
where the time goes in v3:
time: 120 us; the launch traced here: 119 us
  starting transfers between devices  55.3 us (46%)
  waiting for transfers between devices  36 us (30%)
  Pallas kernels  21.5 us (18%)
  local copies, waits for them, and re-layouts  3.18 us (3%)
  other arithmetic  1.96 us (2%)
  between operations  1.49 us (1%)
    ppermute x21, starting transfers between devices, col_permute(): return lax.ppermute(value, 'col', pairs)  33.5 us
    ppermute x21, waiting for transfers between devices, col_permute(): return lax.ppermute(value, 'col', pairs)  24.5 us
    ppermute x3, starting transfers between devices, over_row(): other = lax.ppermute(message, 'row', [(i, i ^ 1) for i in range(8)])  13.9 us
    pallas_call x5, Pallas kernels, call(): pl.pallas_call(body, out_shape=[jax.ShapeDtypeStruct((rows, 128), F32) fo...  11.4 us
    ppermute x9, waiting for transfers between devices, row_permute(): lax.ppermute(value, 'row', [(i, (i + 2 * shift) % 8) for i in range(8)])  8.93 us
    ppermute x9, starting transfers between devices, row_permute(): lax.ppermute(value, 'row', [(i, (i + 2 * shift) % 8) for i in range(8)])  7.85 us
    pallas_call x1, Pallas kernels, first_call(): pl.pallas_call(first_kernel, out_shape=jax.ShapeDtypeStruct((136, 128), F...  5.2 us
    pallas_call x2, Pallas kernels, square_call(): pl.pallas_call(squares, out_shape=SQUARES, in_specs=[SMEM] * 2 + [VMEM] *...  3.58 us
  transfers between devices with their start and end apart: 33, of which 24 were waited for; matrix products, arithmetic and copies ran while one was open for 0% of the time, Pallas kernels for 4%

profile of v3, /device:TPU:1, one launch (start us, length us, event | category | flops | bytes accessed | tf_op | source)
XLA Modules:
  0.0 119.4 jit_solution(6794531979891019014)
XLA Ops:
  1.3 5.2 %shard_map.95 = f32[136,128]{1,0:T(8,128)} custom-call(s32[1,1,64]{2,1,0:T(1,128)} %src_ids.9, s32[1,1,64]{2,1,0:T(1,128)} %tgt_ids.9, s32[1,1]{1,0:T(1,128)S(6)} %copy.10.count_list.count, f32[64,128]{1,0:T(8,128)} %bitcast.15, s32[64,128]{1,0:T(8,128)} %bitcast.12, s32[3,16384]{1,0:T(4,128)} %lane_coords.3, s32[3,8192]{1,0:T(4,128)} %sub_coords.3), custom_call_target="tpu_custom_call" | custom-call | tf_op jit(solution)/shard_map/pallas_call | solution.py:197
  6.5 2.2 %collective-permute-start.2 = (f32[136,128]{1,0:T(8,128)}, f32[136,128]{1,0:T(8,128)S(1)}, u32[]{:S(2)}, u32[]{:S(2)}) collective-permute-start(f32[136,128]{1,0:T(8,128)} %shard_map.95), channel_id=1, source_target_pairs={{8,0},{9,1},{10,2},{11,3},{12,4},{13,5},{14,6},{15,7},{0,8},{1,9},... | collective-permute-start | bytes 208904 | tf_op jit(solution)/shard_map/ppermute | solution.py:244
  8.7 1.5 %collective-permute-start.1 = (f32[136,128]{1,0:T(8,128)}, f32[136,128]{1,0:T(8,128)S(1)}, u32[]{:S(2)}, u32[]{:S(2)}) collective-permute-start(f32[136,128]{1,0:T(8,128)} %shard_map.95), channel_id=1, source_target_pairs={{9,0},{8,1},{11,2},{10,3},{13,4},{12,5},{15,6},{14,7},{1,8},{0,9},... | collective-permute-start | bytes 208904 | tf_op jit(solution)/shard_map/ppermute | solution.py:244
  14.9 3.3 %collective-permute-start.3 = (f32[136,128]{1,0:T(8,128)S(1)}, f32[136,128]{1,0:T(8,128)S(1)}, u32[]{:S(2)}, u32[]{:S(2)}) collective-permute-start(f32[136,128]{1,0:T(8,128)S(1)} %log_add_fusion.1), channel_id=1, source_target_pairs={{24,0},{25,1},{26,2},{27,3},{28,4},{29,5},{30,6},{31,7},{16,8},{17... | collective-permute-start | bytes 208904 | tf_op jit(solution)/shard_map/ppermute | solution.py:244
  19.5 1.8 %shard_map.97.square = f32[64,128,128]{2,1,0:T(8,128)S(1)} custom-call(s32[1,1,64]{2,1,0:T(1,128)S(1)} %copy-done.6, s32[1,1,64]{2,1,0:T(1,128)S(1)} %copy-done.7, bf16[16,128,128]{2,1,0:T(8,128)(2,1)S(1)} %get-tuple-element.24.left_ref, bf16[64,16,128]{2,1,0:T(8,128)(2,1)S(1)} %get-tuple-element.25.right_ref), custom_call_target="tpu_custom_call" | custom-call | tf_op jit(solution)/shard_map/pallas_call | solution.py:219
  21.4 4.7 %collective-permute-start.6 = (f32[136,128]{1,0:T(8,128)S(1)}, f32[136,128]{1,0:T(8,128)S(1)}, u32[]{:S(2)}, u32[]{:S(2)}) collective-permute-start(f32[136,128]{1,0:T(8,128)S(1)} %log_add_fusion.m0), channel_id=1, source_target_pairs={{2,0},{7,1},{4,2},{1,3},{6,4},{3,5},{0,6},{5,7},{10,8},{15,9},{12,... | collective-permute-start | bytes 208904 | tf_op jit(solution)/shard_map/ppermute | solution.py:244
  26.1 1.6 %collective-permute-start.5 = (f32[136,128]{1,0:T(8,128)S(1)}, f32[136,128]{1,0:T(8,128)S(1)}, u32[]{:S(2)}, u32[]{:S(2)}) collective-permute-start(f32[136,128]{1,0:T(8,128)S(1)} %log_add_fusion.m0), channel_id=1, source_target_pairs={{5,0},{4,1},{7,2},{6,3},{1,4},{0,5},{3,6},{2,7},{13,8},{12,9},{15,... | collective-permute-start | bytes 208904 | tf_op jit(solution)/shard_map/ppermute | solution.py:244
  27.9 5.8 %collective-permute-done.5.m2 = f32[136,128]{1,0:T(8,128)S(1)} collective-permute-done((f32[136,128]{1,0:T(8,128)S(1)}, f32[136,128]{1,0:T(8,128)S(1)}, u32[]{:S(2)}, u32[]{:S(2)}) %collective-permute-start.5) | collective-permute-done | bytes 69664 | tf_op jit(solution)/shard_map/ppermute | solution.py:244
  33.7 2.2 %shard_map.99 = (f32[72,128]{1,0:T(8,128)S(1)}, f32[8,128]{1,0:T(8,128)S(1)}) custom-call(s32[1,1,64]{2,1,0:T(1,128)S(1)} %copy-done.6, s32[1,1,64]{2,1,0:T(1,128)S(1)} %copy-done.7, s32[1,1]{1,0:T(1,128)S(6)} %copy.10.count_list.count, f32[136,128]{1,0:T(8,128)S(1)} %log_add_fusion.m0, f32[136,128]{1,0:T(8,128)S(1)} %collective-permute-done.4.m1, ...), custom_call_target="tpu_custom_call" | custom-call | tf_op jit(solution)/shard_map/pallas_call | solution.py:229
  35.9 3.2 %collective-permute-start.7 = (f32[72,128]{1,0:T(8,128)S(1)}, f32[72,128]{1,0:T(8,128)S(1)}, u32[]{:S(2)}, u32[]{:S(2)}) collective-permute-start(f32[72,128]{1,0:T(8,128)S(1)} %get-tuple-element.28), channel_id=1, source_target_pairs={{0,32},{32,0},{64,96},{96,64},{128,160},{160,128},{192,224},{224,1... | collective-permute-start | bytes 110600 | tf_op jit(solution)/shard_map/ppermute | solution.py:267
  40.0 2.5 %collective-permute-start.10 = (f32[72,128]{1,0:T(8,128)S(1)}, f32[72,128]{1,0:T(8,128)S(1)}, u32[]{:S(2)}, u32[]{:S(2)}) collective-permute-start(f32[72,128]{1,0:T(8,128)S(1)} %log_add_fusion.6.m0), channel_id=1, source_target_pairs={{0,192},{32,224},{64,0},{96,32},{128,64},{160,96},{192,128},{224,1... | collective-permute-start | bytes 110600 | tf_op jit(solution)/shard_map/ppermute | solution.py:248
  44.1 1.8 %shard_map.101.square = f32[64,128,128]{2,1,0:T(8,128)S(1)} custom-call(s32[1,1,64]{2,1,0:T(1,128)S(1)} %copy-done.7, s32[1,1,64]{2,1,0:T(1,128)S(1)} %copy-done.6, bf16[8,128,128]{2,1,0:T(8,128)(2,1)S(1)} %get-tuple-element.30.left_ref, bf16[128,16,128]{2,1,0:T(8,128)(2,1)S(1)} %get-tuple-element.31.right_ref), custom_call_target="tpu_custom_call" | custom-call | tf_op jit(solution)/shard_map/pallas_call | solution.py:219
  47.2 2.2 %shard_map.102 = (f32[128,128]{1,0:T(8,128)S(1)}, f32[8,128]{1,0:T(8,128)S(1)}) custom-call(s32[1,1,64]{2,1,0:T(1,128)S(1)} %copy-done.6, s32[1,1,64]{2,1,0:T(1,128)S(1)} %copy-done.7, s32[1,1]{1,0:T(1,128)S(6)} %copy.10.count_list.count, f32[72,128]{1,0:T(8,128)S(1)} %log_add_fusion.6.m0, f32[72,128]{1,0:T(8,128)S(1)} %collective-permute-done.8.m1, ...), custom_call_target="tpu_custom_call" | custom-call | tf_op jit(solution)/shard_map/pallas_call | solution.py:229
  49.8 2.4 %collective-permute-start.11 = (f32[128,128]{1,0:T(8,128)S(1)}, f32[128,128]{1,0:T(8,128)S(1)}, u32[]{:S(2)}, u32[]{:S(2)}) collective-permute-start(f32[128,128]{1,0:T(8,128)S(1)} %get-tuple-element.32), channel_id=1, source_target_pairs={{1,0},{0,1},{3,2},{2,3},{5,4},{4,5},{7,6},{6,7},{9,8},{8,9},{11,10... | collective-permute-start | bytes 196616 | tf_op jit(solution)/shard_map/ppermute | solution.py:244
  53.9 2.7 %collective-permute-start.14 = (f32[128,128]{1,0:T(8,128)S(1)}, f32[128,128]{1,0:T(8,128)S(1)}, u32[]{:S(2)}, u32[]{:S(2)}) collective-permute-start(f32[128,128]{1,0:T(8,128)S(1)} %log_add_fusion.5), channel_id=1, source_target_pairs={{24,0},{25,1},{26,2},{27,3},{28,4},{29,5},{30,6},{31,7},{16,8},{17... | collective-permute-start | bytes 196616 | tf_op jit(solution)/shard_map/ppermute | solution.py:244
  56.6 1.7 %collective-permute-done.14 = f32[128,128]{1,0:T(8,128)S(1)} collective-permute-done((f32[128,128]{1,0:T(8,128)S(1)}, f32[128,128]{1,0:T(8,128)S(1)}, u32[]{:S(2)}, u32[]{:S(2)}) %collective-permute-start.14) | collective-permute-done | bytes 65568 | tf_op jit(solution)/shard_map/ppermute | solution.py:244
  58.4 1.8 %collective-permute-start.17 = (f32[128,128]{1,0:T(8,128)S(1)}, f32[128,128]{1,0:T(8,128)S(1)}, u32[]{:S(2)}, u32[]{:S(2)}) collective-permute-start(f32[128,128]{1,0:T(8,128)S(1)} %log_add_fusion.4.m0), channel_id=1, source_target_pairs={{2,0},{7,1},{4,2},{1,3},{6,4},{3,5},{0,6},{5,7},{10,8},{15,9},{12,... | collective-permute-start | bytes 196616 | tf_op jit(solution)/shard_map/ppermute | solution.py:244
  60.1 2.0 %collective-permute-start.16 = (f32[128,128]{1,0:T(8,128)S(1)}, f32[128,128]{1,0:T(8,128)S(1)}, u32[]{:S(2)}, u32[]{:S(2)}) collective-permute-start(f32[128,128]{1,0:T(8,128)S(1)} %log_add_fusion.4.m0), channel_id=1, source_target_pairs={{5,0},{4,1},{7,2},{6,3},{1,4},{0,5},{3,6},{2,7},{13,8},{12,9},{15,... | collective-permute-start | bytes 196616 | tf_op jit(solution)/shard_map/ppermute | solution.py:244
  63.2 3.1 %collective-permute-done.16.m2 = f32[128,128]{1,0:T(8,128)S(1)} collective-permute-done((f32[128,128]{1,0:T(8,128)S(1)}, f32[128,128]{1,0:T(8,128)S(1)}, u32[]{:S(2)}, u32[]{:S(2)}) %collective-permute-start.16) | collective-permute-done | bytes 65568 | tf_op jit(solution)/shard_map/ppermute | solution.py:244
  67.1 2.2 %shard_map.103 = f32[64,128]{1,0:T(8,128)S(1)} custom-call(s32[1,1,64]{2,1,0:T(1,128)S(1)} %copy-done.6, s32[1,1,64]{2,1,0:T(1,128)S(1)} %copy-done.7, s32[1,1]{1,0:T(1,128)S(6)} %copy.10.count_list.count, f32[128,128]{1,0:T(8,128)S(1)} %log_add_fusion.4.m0, f32[128,128]{1,0:T(8,128)S(1)} %collective-permute-done.15.m1, ...), custom_call_target="tpu_custom_call" | custom-call | tf_op jit(solution)/shard_map/pallas_call | solution.py:229
  69.2 5.8 %collective-permute-start.18 = (f32[64,128]{1,0:T(8,128)S(1)}, f32[64,128]{1,0:T(8,128)S(1)}, u32[]{:S(2)}, u32[]{:S(2)}) collective-permute-start(f32[64,128]{1,0:T(8,128)S(1)} %shard_map.103), channel_id=1, source_target_pairs={{0,32},{32,0},{64,96},{96,64},{128,160},{160,128},{192,224},{224,1... | collective-permute-start | bytes 98312 | tf_op jit(solution)/shard_map/ppermute | solution.py:267
  78.8 1.7 %collective-permute-done.20.m2 = f32[64,128]{1,0:T(8,128)S(1)} collective-permute-done((f32[64,128]{1,0:T(8,128)S(1)}, f32[64,128]{1,0:T(8,128)S(1)}, u32[]{:S(2)}, u32[]{:S(2)}) %collective-permute-start.20) | collective-permute-done | bytes 32800 | tf_op jit(solution)/shard_map/ppermute | solution.py:248
  81.9 2.2 %shard_map.104 = f32[128,128]{1,0:T(8,128)S(1)} custom-call(s32[1,1,64]{2,1,0:T(1,128)S(1)} %copy-done.6, s32[1,1,64]{2,1,0:T(1,128)S(1)} %copy-done.7, s32[1,1]{1,0:T(1,128)S(6)} %copy.10.count_list.count, f32[64,128]{1,0:T(8,128)S(1)} %log_add_fusion.8.m0, f32[64,128]{1,0:T(8,128)S(1)} %collective-permute-done.19.m1, ...), custom_call_target="tpu_custom_call" | custom-call | tf_op jit(solution)/shard_map/pallas_call | solution.py:229
  84.2 2.1 %collective-permute-start.23 = (f32[128,128]{1,0:T(8,128)S(1)}, f32[128,128]{1,0:T(8,128)S(1)}, u32[]{:S(2)}, u32[]{:S(2)}) collective-permute-start(f32[128,128]{1,0:T(8,128)S(1)} %shard_map.104), channel_id=1, source_target_pairs={{8,0},{9,1},{10,2},{11,3},{12,4},{13,5},{14,6},{15,7},{0,8},{1,9},... | collective-permute-start | bytes 196616 | tf_op jit(solution)/shard_map/ppermute | solution.py:244
  89.7 2.2 %collective-permute-start.25 = (f32[128,128]{1,0:T(8,128)S(1)}, f32[128,128]{1,0:T(8,128)S(1)}, u32[]{:S(2)}, u32[]{:S(2)}) collective-permute-start(f32[128,128]{1,0:T(8,128)S(1)} %log_add_fusion.3), channel_id=1, source_target_pairs={{24,0},{25,1},{26,2},{27,3},{28,4},{29,5},{30,6},{31,7},{16,8},{17... | collective-permute-start | bytes 196616 | tf_op jit(solution)/shard_map/ppermute | solution.py:244
  91.9 2.2 %collective-permute-done.25 = f32[128,128]{1,0:T(8,128)S(1)} collective-permute-done((f32[128,128]{1,0:T(8,128)S(1)}, f32[128,128]{1,0:T(8,128)S(1)}, u32[]{:S(2)}, u32[]{:S(2)}) %collective-permute-start.25) | collective-permute-done | bytes 65568 | tf_op jit(solution)/shard_map/ppermute | solution.py:244
  94.2 2.7 %collective-permute-start.28 = (f32[128,128]{1,0:T(8,128)S(1)}, f32[128,128]{1,0:T(8,128)S(1)}, u32[]{:S(2)}, u32[]{:S(2)}) collective-permute-start(f32[128,128]{1,0:T(8,128)S(1)} %log_add_fusion.2.m0), channel_id=1, source_target_pairs={{2,0},{7,1},{4,2},{1,3},{6,4},{3,5},{0,6},{5,7},{10,8},{15,9},{12,... | collective-permute-start | bytes 196616 | tf_op jit(solution)/shard_map/ppermute | solution.py:244
  97.6 1.5 %collective-permute-start.26 = (f32[128,128]{1,0:T(8,128)S(1)}, f32[128,128]{1,0:T(8,128)S(1)}, u32[]{:S(2)}, u32[]{:S(2)}) collective-permute-start(f32[128,128]{1,0:T(8,128)S(1)} %log_add_fusion.2.m0), channel_id=1, source_target_pairs={{7,0},{2,1},{1,2},{4,3},{3,4},{6,5},{5,6},{0,7},{15,8},{10,9},{9,1... | collective-permute-start | bytes 196616 | tf_op jit(solution)/shard_map/ppermute | solution.py:244
  99.0 5.3 %collective-permute-done.27.m2 = f32[128,128]{1,0:T(8,128)S(1)} collective-permute-done((f32[128,128]{1,0:T(8,128)S(1)}, f32[128,128]{1,0:T(8,128)S(1)}, u32[]{:S(2)}, u32[]{:S(2)}) %collective-permute-start.27) | collective-permute-done | bytes 65568 | tf_op jit(solution)/shard_map/ppermute | solution.py:244
  104.3 2.7 %shard_map.105 = (f32[64,128]{1,0:T(8,128)S(1)}, f32[128,128]{1,0:T(8,128)}) custom-call(s32[1,1,64]{2,1,0:T(1,128)S(1)} %copy-done.6, s32[1,1,64]{2,1,0:T(1,128)S(1)} %copy-done.7, s32[1,1]{1,0:T(1,128)S(6)} %copy.10.count_list.count, f32[128,128]{1,0:T(8,128)S(1)} %log_add_fusion.2.m0, f32[128,128]{1,0:T(8,128)S(1)} %collective-permute-done.26.m1, ...), custom_call_target="tpu_custom_call" | custom-call | tf_op jit(solution)/shard_map/pallas_call | solution.py:229
  107.0 4.9 %collective-permute-start.29 = (f32[64,128]{1,0:T(8,128)S(1)}, f32[64,128]{1,0:T(8,128)S(1)}, u32[]{:S(2)}, u32[]{:S(2)}) collective-permute-start(f32[64,128]{1,0:T(8,128)S(1)} %get-tuple-element.35), channel_id=1, source_target_pairs={{0,32},{32,0},{64,96},{96,64},{128,160},{160,128},{192,224},{224,1... | collective-permute-start | bytes 98312 | tf_op jit(solution)/shard_map/ppermute | solution.py:267
  115.6 2.8 %collective-permute-done.31 = f32[64,128]{1,0:T(8,128)S(1)} collective-permute-done((f32[64,128]{1,0:T(8,128)S(1)}, f32[64,128]{1,0:T(8,128)S(1)}, u32[]{:S(2)}, u32[]{:S(2)}) %collective-permute-start.31) | collective-permute-done | bytes 32800 | tf_op jit(solution)/shard_map/ppermute | solution.py:248
  (72 shorter events, 28.0 us)
Async XLA Ops:
  6.5 6.3 %collective-permute-start.2 = (f32[136,128]{1,0:T(8,128)}, f32[136,128]{1,0:T(8,128)S(1)}, u32[]{:S(2)}, u32[]{:S(2)}) collective-permute-start(f32[136,128]{1,0:T(8,128)} %shard_map.95), channel_id=1, source_target_pairs={{8,0},{9,1},{10,2},{11,3},{12,4},{13,5},{14,6},{15,7},{0,8},{1,9},... | collective-permute-start | bytes 208904 | tf_op jit(solution)/shard_map/ppermute | solution.py:244
  8.7 4.3 %collective-permute-start.1 = (f32[136,128]{1,0:T(8,128)}, f32[136,128]{1,0:T(8,128)S(1)}, u32[]{:S(2)}, u32[]{:S(2)}) collective-permute-start(f32[136,128]{1,0:T(8,128)} %shard_map.95), channel_id=1, source_target_pairs={{9,0},{8,1},{11,2},{10,3},{13,4},{12,5},{15,6},{14,7},{1,8},{0,9},... | collective-permute-start | bytes 208904 | tf_op jit(solution)/shard_map/ppermute | solution.py:244
  10.3 3.7 %collective-permute-start = (f32[136,128]{1,0:T(8,128)}, f32[136,128]{1,0:T(8,128)S(1)}, u32[]{:S(2)}, u32[]{:S(2)}) collective-permute-start(f32[136,128]{1,0:T(8,128)} %shard_map.95), channel_id=1, source_target_pairs={{1,0},{0,1},{3,2},{2,3},{5,4},{4,5},{7,6},{6,7},{9,8},{8,9},{11,10... | collective-permute-start | bytes 208904 | tf_op jit(solution)/shard_map/ppermute | solution.py:244
  14.9 6.4 %collective-permute-start.3 = (f32[136,128]{1,0:T(8,128)S(1)}, f32[136,128]{1,0:T(8,128)S(1)}, u32[]{:S(2)}, u32[]{:S(2)}) collective-permute-start(f32[136,128]{1,0:T(8,128)S(1)} %log_add_fusion.1), channel_id=1, source_target_pairs={{24,0},{25,1},{26,2},{27,3},{28,4},{29,5},{30,6},{31,7},{16,8},{17... | collective-permute-start | bytes 208904 | tf_op jit(solution)/shard_map/ppermute | solution.py:244
  21.4 6.5 %collective-permute-start.6 = (f32[136,128]{1,0:T(8,128)S(1)}, f32[136,128]{1,0:T(8,128)S(1)}, u32[]{:S(2)}, u32[]{:S(2)}) collective-permute-start(f32[136,128]{1,0:T(8,128)S(1)} %log_add_fusion.m0), channel_id=1, source_target_pairs={{2,0},{7,1},{4,2},{1,3},{6,4},{3,5},{0,6},{5,7},{10,8},{15,9},{12,... | collective-permute-start | bytes 208904 | tf_op jit(solution)/shard_map/ppermute | solution.py:244
  26.1 7.6 %collective-permute-start.5 = (f32[136,128]{1,0:T(8,128)S(1)}, f32[136,128]{1,0:T(8,128)S(1)}, u32[]{:S(2)}, u32[]{:S(2)}) collective-permute-start(f32[136,128]{1,0:T(8,128)S(1)} %log_add_fusion.m0), channel_id=1, source_target_pairs={{5,0},{4,1},{7,2},{6,3},{1,4},{0,5},{3,6},{2,7},{13,8},{12,9},{15,... | collective-permute-start | bytes 208904 | tf_op jit(solution)/shard_map/ppermute | solution.py:244
  27.7 6.0 %collective-permute-start.4 = (f32[136,128]{1,0:T(8,128)S(1)}, f32[136,128]{1,0:T(8,128)S(1)}, u32[]{:S(2)}, u32[]{:S(2)}) collective-permute-start(f32[136,128]{1,0:T(8,128)S(1)} %log_add_fusion.m0), channel_id=1, source_target_pairs={{7,0},{2,1},{1,2},{4,3},{3,4},{6,5},{5,6},{0,7},{15,8},{10,9},{9,1... | collective-permute-start | bytes 208904 | tf_op jit(solution)/shard_map/ppermute | solution.py:244
  35.9 4.0 %collective-permute-start.7 = (f32[72,128]{1,0:T(8,128)S(1)}, f32[72,128]{1,0:T(8,128)S(1)}, u32[]{:S(2)}, u32[]{:S(2)}) collective-permute-start(f32[72,128]{1,0:T(8,128)S(1)} %get-tuple-element.28), channel_id=1, source_target_pairs={{0,32},{32,0},{64,96},{96,64},{128,160},{160,128},{192,224},{224,1... | collective-permute-start | bytes 110600 | tf_op jit(solution)/shard_map/ppermute | solution.py:267
  40.0 6.0 %collective-permute-start.10 = (f32[72,128]{1,0:T(8,128)S(1)}, f32[72,128]{1,0:T(8,128)S(1)}, u32[]{:S(2)}, u32[]{:S(2)}) collective-permute-start(f32[72,128]{1,0:T(8,128)S(1)} %log_add_fusion.6.m0), channel_id=1, source_target_pairs={{0,192},{32,224},{64,0},{96,32},{128,64},{160,96},{192,128},{224,1... | collective-permute-start | bytes 110600 | tf_op jit(solution)/shard_map/ppermute | solution.py:248
  42.5 4.3 %collective-permute-start.9 = (f32[72,128]{1,0:T(8,128)S(1)}, f32[72,128]{1,0:T(8,128)S(1)}, u32[]{:S(2)}, u32[]{:S(2)}) collective-permute-start(f32[72,128]{1,0:T(8,128)S(1)} %log_add_fusion.6.m0), channel_id=1, source_target_pairs={{0,128},{32,160},{64,192},{96,224},{128,0},{160,32},{192,64},{224,... | collective-permute-start | bytes 110600 | tf_op jit(solution)/shard_map/ppermute | solution.py:248
  43.0 4.2 %collective-permute-start.8 = (f32[72,128]{1,0:T(8,128)S(1)}, f32[72,128]{1,0:T(8,128)S(1)}, u32[]{:S(2)}, u32[]{:S(2)}) collective-permute-start(f32[72,128]{1,0:T(8,128)S(1)} %log_add_fusion.6.m0), channel_id=1, source_target_pairs={{0,64},{32,96},{64,128},{96,160},{128,192},{160,224},{192,0},{224,... | collective-permute-start | bytes 110600 | tf_op jit(solution)/shard_map/ppermute | solution.py:248
  49.4 4.1 %collective-permute-start.13 = (f32[128,128]{1,0:T(8,128)S(1)}, f32[128,128]{1,0:T(8,128)S(1)}, u32[]{:S(2)}, u32[]{:S(2)}) collective-permute-start(f32[128,128]{1,0:T(8,128)S(1)} %get-tuple-element.32), channel_id=1, source_target_pairs={{9,0},{8,1},{11,2},{10,3},{13,4},{12,5},{15,6},{14,7},{1,8},{0,9},... | collective-permute-start | bytes 196616 | tf_op jit(solution)/shard_map/ppermute | solution.py:244
  49.5 4.0 %collective-permute-start.12 = (f32[128,128]{1,0:T(8,128)S(1)}, f32[128,128]{1,0:T(8,128)S(1)}, u32[]{:S(2)}, u32[]{:S(2)}) collective-permute-start(f32[128,128]{1,0:T(8,128)S(1)} %get-tuple-element.32), channel_id=1, source_target_pairs={{8,0},{9,1},{10,2},{11,3},{12,4},{13,5},{14,6},{15,7},{0,8},{1,9},... | collective-permute-start | bytes 196616 | tf_op jit(solution)/shard_map/ppermute | solution.py:244
  49.8 4.1 %collective-permute-start.11 = (f32[128,128]{1,0:T(8,128)S(1)}, f32[128,128]{1,0:T(8,128)S(1)}, u32[]{:S(2)}, u32[]{:S(2)}) collective-permute-start(f32[128,128]{1,0:T(8,128)S(1)} %get-tuple-element.32), channel_id=1, source_target_pairs={{1,0},{0,1},{3,2},{2,3},{5,4},{4,5},{7,6},{6,7},{9,8},{8,9},{11,10... | collective-permute-start | bytes 196616 | tf_op jit(solution)/shard_map/ppermute | solution.py:244
  53.9 4.4 %collective-permute-start.14 = (f32[128,128]{1,0:T(8,128)S(1)}, f32[128,128]{1,0:T(8,128)S(1)}, u32[]{:S(2)}, u32[]{:S(2)}) collective-permute-start(f32[128,128]{1,0:T(8,128)S(1)} %log_add_fusion.5), channel_id=1, source_target_pairs={{24,0},{25,1},{26,2},{27,3},{28,4},{29,5},{30,6},{31,7},{16,8},{17... | collective-permute-start | bytes 196616 | tf_op jit(solution)/shard_map/ppermute | solution.py:244
  58.4 4.8 %collective-permute-start.17 = (f32[128,128]{1,0:T(8,128)S(1)}, f32[128,128]{1,0:T(8,128)S(1)}, u32[]{:S(2)}, u32[]{:S(2)}) collective-permute-start(f32[128,128]{1,0:T(8,128)S(1)} %log_add_fusion.4.m0), channel_id=1, source_target_pairs={{2,0},{7,1},{4,2},{1,3},{6,4},{3,5},{0,6},{5,7},{10,8},{15,9},{12,... | collective-permute-start | bytes 196616 | tf_op jit(solution)/shard_map/ppermute | solution.py:244
  60.1 6.2 %collective-permute-start.16 = (f32[128,128]{1,0:T(8,128)S(1)}, f32[128,128]{1,0:T(8,128)S(1)}, u32[]{:S(2)}, u32[]{:S(2)}) collective-permute-start(f32[128,128]{1,0:T(8,128)S(1)} %log_add_fusion.4.m0), channel_id=1, source_target_pairs={{5,0},{4,1},{7,2},{6,3},{1,4},{0,5},{3,6},{2,7},{13,8},{12,9},{15,... | collective-permute-start | bytes 196616 | tf_op jit(solution)/shard_map/ppermute | solution.py:244
  62.1 5.0 %collective-permute-start.15 = (f32[128,128]{1,0:T(8,128)S(1)}, f32[128,128]{1,0:T(8,128)S(1)}, u32[]{:S(2)}, u32[]{:S(2)}) collective-permute-start(f32[128,128]{1,0:T(8,128)S(1)} %log_add_fusion.4.m0), channel_id=1, source_target_pairs={{7,0},{2,1},{1,2},{4,3},{3,4},{6,5},{5,6},{0,7},{15,8},{10,9},{9,1... | collective-permute-start | bytes 196616 | tf_op jit(solution)/shard_map/ppermute | solution.py:244
  69.2 6.7 %collective-permute-start.18 = (f32[64,128]{1,0:T(8,128)S(1)}, f32[64,128]{1,0:T(8,128)S(1)}, u32[]{:S(2)}, u32[]{:S(2)}) collective-permute-start(f32[64,128]{1,0:T(8,128)S(1)} %shard_map.103), channel_id=1, source_target_pairs={{0,32},{32,0},{64,96},{96,64},{128,160},{160,128},{192,224},{224,1... | collective-permute-start | bytes 98312 | tf_op jit(solution)/shard_map/ppermute | solution.py:267
  76.0 2.8 %collective-permute-start.21 = (f32[64,128]{1,0:T(8,128)S(1)}, f32[64,128]{1,0:T(8,128)S(1)}, u32[]{:S(2)}, u32[]{:S(2)}) collective-permute-start(f32[64,128]{1,0:T(8,128)S(1)} %log_add_fusion.8.m0), channel_id=1, source_target_pairs={{0,192},{32,224},{64,0},{96,32},{128,64},{160,96},{192,128},{224,1... | collective-permute-start | bytes 98312 | tf_op jit(solution)/shard_map/ppermute | solution.py:248
  76.2 4.3 %collective-permute-start.20 = (f32[64,128]{1,0:T(8,128)S(1)}, f32[64,128]{1,0:T(8,128)S(1)}, u32[]{:S(2)}, u32[]{:S(2)}) collective-permute-start(f32[64,128]{1,0:T(8,128)S(1)} %log_add_fusion.8.m0), channel_id=1, source_target_pairs={{0,128},{32,160},{64,192},{96,224},{128,0},{160,32},{192,64},{224,... | collective-permute-start | bytes 98312 | tf_op jit(solution)/shard_map/ppermute | solution.py:248
  77.4 4.5 %collective-permute-start.19 = (f32[64,128]{1,0:T(8,128)S(1)}, f32[64,128]{1,0:T(8,128)S(1)}, u32[]{:S(2)}, u32[]{:S(2)}) collective-permute-start(f32[64,128]{1,0:T(8,128)S(1)} %log_add_fusion.8.m0), channel_id=1, source_target_pairs={{0,64},{32,96},{64,128},{96,160},{128,192},{160,224},{192,0},{224,... | collective-permute-start | bytes 98312 | tf_op jit(solution)/shard_map/ppermute | solution.py:248
  84.1 4.2 %collective-permute-start.24 = (f32[128,128]{1,0:T(8,128)S(1)}, f32[128,128]{1,0:T(8,128)S(1)}, u32[]{:S(2)}, u32[]{:S(2)}) collective-permute-start(f32[128,128]{1,0:T(8,128)S(1)} %shard_map.104), channel_id=1, source_target_pairs={{9,0},{8,1},{11,2},{10,3},{13,4},{12,5},{15,6},{14,7},{1,8},{0,9},... | collective-permute-start | bytes 196616 | tf_op jit(solution)/shard_map/ppermute | solution.py:244
  84.2 4.4 %collective-permute-start.23 = (f32[128,128]{1,0:T(8,128)S(1)}, f32[128,128]{1,0:T(8,128)S(1)}, u32[]{:S(2)}, u32[]{:S(2)}) collective-permute-start(f32[128,128]{1,0:T(8,128)S(1)} %shard_map.104), channel_id=1, source_target_pairs={{8,0},{9,1},{10,2},{11,3},{12,4},{13,5},{14,6},{15,7},{0,8},{1,9},... | collective-permute-start | bytes 196616 | tf_op jit(solution)/shard_map/ppermute | solution.py:244
  86.3 3.4 %collective-permute-start.22 = (f32[128,128]{1,0:T(8,128)S(1)}, f32[128,128]{1,0:T(8,128)S(1)}, u32[]{:S(2)}, u32[]{:S(2)}) collective-permute-start(f32[128,128]{1,0:T(8,128)S(1)} %shard_map.104), channel_id=1, source_target_pairs={{1,0},{0,1},{3,2},{2,3},{5,4},{4,5},{7,6},{6,7},{9,8},{8,9},{11,10... | collective-permute-start | bytes 196616 | tf_op jit(solution)/shard_map/ppermute | solution.py:244
  89.7 4.4 %collective-permute-start.25 = (f32[128,128]{1,0:T(8,128)S(1)}, f32[128,128]{1,0:T(8,128)S(1)}, u32[]{:S(2)}, u32[]{:S(2)}) collective-permute-start(f32[128,128]{1,0:T(8,128)S(1)} %log_add_fusion.3), channel_id=1, source_target_pairs={{24,0},{25,1},{26,2},{27,3},{28,4},{29,5},{30,6},{31,7},{16,8},{17... | collective-permute-start | bytes 196616 | tf_op jit(solution)/shard_map/ppermute | solution.py:244
  94.2 4.8 %collective-permute-start.28 = (f32[128,128]{1,0:T(8,128)S(1)}, f32[128,128]{1,0:T(8,128)S(1)}, u32[]{:S(2)}, u32[]{:S(2)}) collective-permute-start(f32[128,128]{1,0:T(8,128)S(1)} %log_add_fusion.2.m0), channel_id=1, source_target_pairs={{2,0},{7,1},{4,2},{1,3},{6,4},{3,5},{0,6},{5,7},{10,8},{15,9},{12,... | collective-permute-start | bytes 196616 | tf_op jit(solution)/shard_map/ppermute | solution.py:244
  96.9 7.4 %collective-permute-start.27 = (f32[128,128]{1,0:T(8,128)S(1)}, f32[128,128]{1,0:T(8,128)S(1)}, u32[]{:S(2)}, u32[]{:S(2)}) collective-permute-start(f32[128,128]{1,0:T(8,128)S(1)} %log_add_fusion.2.m0), channel_id=1, source_target_pairs={{5,0},{4,1},{7,2},{6,3},{1,4},{0,5},{3,6},{2,7},{13,8},{12,9},{15,... | collective-permute-start | bytes 196616 | tf_op jit(solution)/shard_map/ppermute | solution.py:244
  97.6 6.8 %collective-permute-start.26 = (f32[128,128]{1,0:T(8,128)S(1)}, f32[128,128]{1,0:T(8,128)S(1)}, u32[]{:S(2)}, u32[]{:S(2)}) collective-permute-start(f32[128,128]{1,0:T(8,128)S(1)} %log_add_fusion.2.m0), channel_id=1, source_target_pairs={{7,0},{2,1},{1,2},{4,3},{3,4},{6,5},{5,6},{0,7},{15,8},{10,9},{9,1... | collective-permute-start | bytes 196616 | tf_op jit(solution)/shard_map/ppermute | solution.py:244
  107.0 5.7 %collective-permute-start.29 = (f32[64,128]{1,0:T(8,128)S(1)}, f32[64,128]{1,0:T(8,128)S(1)}, u32[]{:S(2)}, u32[]{:S(2)}) collective-permute-start(f32[64,128]{1,0:T(8,128)S(1)} %get-tuple-element.35), channel_id=1, source_target_pairs={{0,32},{32,0},{64,96},{96,64},{128,160},{160,128},{192,224},{224,1... | collective-permute-start | bytes 98312 | tf_op jit(solution)/shard_map/ppermute | solution.py:267
  114.1 4.3 %collective-permute-start.31 = (f32[64,128]{1,0:T(8,128)S(1)}, f32[64,128]{1,0:T(8,128)S(1)}, u32[]{:S(2)}, u32[]{:S(2)}) collective-permute-start(f32[64,128]{1,0:T(8,128)S(1)} %log_add_fusion.7), channel_id=1, source_target_pairs={{0,128},{32,160},{64,192},{96,224},{128,0},{160,32},{192,64},{224,... | collective-permute-start | bytes 98312 | tf_op jit(solution)/shard_map/ppermute | solution.py:248
  114.7 4.0 %collective-permute-start.30 = (f32[64,128]{1,0:T(8,128)S(1)}, f32[64,128]{1,0:T(8,128)S(1)}, u32[]{:S(2)}, u32[]{:S(2)}) collective-permute-start(f32[64,128]{1,0:T(8,128)S(1)} %log_add_fusion.7), channel_id=1, source_target_pairs={{0,64},{32,96},{64,128},{96,160},{128,192},{160,224},{192,0},{224,... | collective-permute-start | bytes 98312 | tf_op jit(solution)/shard_map/ppermute | solution.py:248
  (9 other events, 97.3 us)
